TPU v7x, 256 devices: a whole 4x4x8 slice. The times are simulated.
256 devices in a mesh: vertex: 64 (over x, y_lo, z), feat: 4 (over y_hi, core).
Axes of the slice: x: 4, y: 4 (y_hi: 2, y_lo: 2; y = y_hi * 2 + y_lo), z: 8, core: 2. Of those that a mesh axis runs over, the one named last changes fastest.
Arguments:
- features: bfloat16 [196608, 512], P('vertex', 'feat'), may hold values from -6 to 6
- tiles: bfloat16 [24576, 128, 128], P('vertex'), as said below
- tile_row: int32 [24576], P('vertex'), may hold values from 0 to 24, as said below
- tile_col: int32 [24576], P('vertex'), may hold values from 0 to 1535, as said below
- permutation: int32 [196608], P('vertex'), may hold values from 0 to 196607, as said below
- weight: bfloat16 [512, 512], P('feat'), may hold values from -0.25 to 0.25
- cotangent: bfloat16 [196608, 512], P('vertex', 'feat'), may hold values from -6 to 6
Outputs:
- activations: bfloat16 [196608, 512], P('vertex', 'feat')
- grad_features: bfloat16 [196608, 512], P('vertex', 'feat')
- grad_weight: float32 [512, 512], P('feat')
Inputs may be any that keep to these rules, and one draw needn't show every extreme that they name: `tile_row`: the live slots of a device come first; a slot with row 24 is empty and its tile is zero; some device has all 384 slots live in every draw. `tile_col`: every tile's column block lies on a device at most 3 positions away from the tile's own device around the vertex axis, wrapping at its ends; an empty slot names its device's first block. Empty slots hold zero tiles. Each device's 24 * 128 consecutive entries are a permutation of that device's own node numbers.
All inputs are finite; a program needn't handle non-finite values.
Results may differ from a plain program's by a relative error of at most 0.0061.
Values may be sent and summed in bfloat16 or wider, within the bound.
No kernel may reach another device: no remote copies, remote signals or barrier semaphores. Data moves between devices by JAX's collectives and lax.ppermute only.
A program may use at most 128 MiB of HBM per device.

v0:
```python
import math

import jax
import jax.numpy as jnp
from jax import lax
from jax.sharding import PartitionSpec as P

REACH = 3


slots_per_step = 32


def from_behind(value, axis, steps):
    count = lax.axis_size(axis)
    pairs = [(source, (source + steps) % count) for source in range(count)]
    return lax.ppermute(value, axis, pairs)


def body(features, tiles, tile_row, tile_col, permutation, weight, cotangent):
    rows, width = features.shape
    side = tiles.shape[1]
    blocks = rows // side
    devices = lax.axis_size("vertex")
    here = lax.axis_index("vertex")
    local_perm = permutation - here * rows
    ordered = jnp.take(features, local_perm, axis=0)
    pieces = []
    for offset in range(-REACH, REACH + 1):
        if offset == 0:
            pieces.append(ordered)
        else:
            pieces.append(from_behind(ordered, "vertex", -offset))
    window_blocks = jnp.concatenate(pieces, axis=0).reshape((2 * REACH + 1) * blocks, side, width)
    owner = tile_col // blocks
    window_index = (owner - here + REACH + devices) % devices * blocks + tile_col % blocks
    live = jnp.sum((tile_row < blocks).astype(jnp.int32))
    turns = (live + slots_per_step - 1) // slots_per_step

    def forward_step(turn, total):
        start = turn * slots_per_step
        tile_g = lax.dynamic_slice_in_dim(tiles, start, slots_per_step, 0)
        row_g = lax.dynamic_slice_in_dim(tile_row, start, slots_per_step, 0)
        win_g = lax.dynamic_slice_in_dim(window_index, start, slots_per_step, 0)
        source = jnp.take(window_blocks, win_g, axis=0)
        product = jnp.einsum("tij,tjf->tif", tile_g, source, preferred_element_type=jnp.float32)
        return total.at[row_g].add(product)

    summed = lax.fori_loop(
        0, turns, forward_step, jnp.zeros((blocks + 1, side, width), jnp.float32)
    )
    aggregated = summed[:blocks].reshape(rows, width).astype(jnp.bfloat16)
    terms = jnp.dot(aggregated, weight, preferred_element_type=jnp.float32)
    mixed = lax.psum_scatter(terms, "feat", scatter_dimension=1, tiled=True)
    activations = jax.nn.silu(mixed).astype(jnp.bfloat16)
    sig = jax.nn.sigmoid(mixed)
    grad_mixed = (cotangent.astype(jnp.float32) * sig * (1.0 + mixed * (1.0 - sig))).astype(
        jnp.bfloat16
    )
    grad_full = lax.all_gather(grad_mixed, "feat", axis=1, tiled=True)
    weight_terms = lax.dot_general(
        aggregated, grad_full, (((0,), (0,)), ((), ())), preferred_element_type=jnp.float32
    )
    grad_weight = lax.psum(weight_terms, "vertex") * (1.0 / math.sqrt(rows * devices))
    grad_aggregated = lax.dot_general(
        grad_full, weight, (((1,), (1,)), ((), ())), preferred_element_type=jnp.float32
    ).astype(jnp.bfloat16)
    grad_blocks = grad_aggregated.reshape(blocks, side, width)

    def backward_step(turn, partial_value):
        start = turn * slots_per_step
        tile_g = lax.dynamic_slice_in_dim(tiles, start, slots_per_step, 0)
        row_g = lax.dynamic_slice_in_dim(tile_row, start, slots_per_step, 0)
        win_g = lax.dynamic_slice_in_dim(window_index, start, slots_per_step, 0)
        source = jnp.take(grad_blocks, jnp.minimum(row_g, blocks - 1), axis=0)
        contrib = jnp.einsum("tji,tjf->tif", tile_g, source, preferred_element_type=jnp.float32)
        return partial_value.at[win_g].add(contrib)

    partial_value = lax.fori_loop(
        0, turns, backward_step, jnp.zeros(((2 * REACH + 1) * blocks, side, width), jnp.float32)
    )
    segments = partial_value.reshape(2 * REACH + 1, blocks, side, width)
    total = segments[REACH]
    for offset in range(-REACH, REACH + 1):
        if offset != 0:
            total = total + from_behind(segments[REACH + offset], "vertex", offset)
    grad_ordered = total.reshape(rows, width).astype(jnp.bfloat16)
    grad_features = jnp.zeros((rows, width), jnp.bfloat16).at[local_perm].set(grad_ordered)
    return (activations, grad_features, grad_weight)


def solution(mesh):
    in_specs = (
        P("vertex", "feat"),
        P("vertex", None, None),
        P("vertex"),
        P("vertex"),
        P("vertex"),
        P("feat", None),
        P("vertex", "feat"),
    )
    out_specs = (P("vertex", "feat"), P("vertex", "feat"), P("feat", None))
    return jax.shard_map(body, mesh=mesh, in_specs=in_specs, out_specs=out_specs, check_vma=False)
```

profile of v0, /device:TPU:16, one launch (start us, length us, event | category | flops | bytes accessed | tf_op | source)
XLA Modules:
  0.0 1192.3 jit_solution(3282797562533588028)
XLA Ops:
  8.3 9.2 gather_fusion.2
  17.5 2.3 broadcast_select_fusion
  19.8 4.6 collective-permute-start
  24.4 3.6 collective-permute-start.1
  28.0 3.1 collective-permute-start.5
  31.1 2.9 collective-permute-start.4
  36.1 45.3 %collective-permute-done = bf16[3072,128]{1,0:T(8,128)(2,1)} collective-permute-done((bf16[3072,128]{1,0:T(8,128)(2,1)}, bf16[3072,128]{1,0:T(8,128)(2,1)}, u32[]{:S(2)}, u32[]{:S(2)}) %collective-permute-start) | collective-permute-done | bytes 786464 | tf_op jit(solution)/shard_map/ppermute | solution.py:17
  81.4 2.8 collective-permute-start.3
  85.4 26.7 %collective-permute-done.1 = bf16[3072,128]{1,0:T(8,128)(2,1)S(1)} collective-permute-done((bf16[3072,128]{1,0:T(8,128)(2,1)}, bf16[3072,128]{1,0:T(8,128)(2,1)S(1)}, u32[]{:S(2)}, u32[]{:S(2)}) %collective-permute-start.1) | collective-permute-done | bytes 786464 | tf_op jit(solution)/shard_map/ppermute | solution.py:17
  112.2 18.6 %collective-permute-done.2 = bf16[3072,128]{1,0:T(8,128)(2,1)} collective-permute-done((bf16[3072,128]{1,0:T(8,128)(2,1)}, bf16[3072,128]{1,0:T(8,128)(2,1)}, u32[]{:S(2)}, u32[]{:S(2)}) %collective-permute-start.2) | collective-permute-done | bytes 786464 | tf_op jit(solution)/shard_map/ppermute | solution.py:17
  132.1 1.9 constant_dynamic-update-slice_fusion.3
  137.3 45.4 %while.20 = (s32[]{:T(128)}, f32[25,128,128]{2,1,0:T(8,128)}, s32[]{:T(128)}, s32[384]{0:T(512)S(1)}, bf16[384,128,128]{2,1,0:T(8,128)(2,1)}, /*index=5*/s32[384...) while((s32[]{:T(128)}, f32[25,128,128]{2,1,0:T(8,128)}, ...), condition=%wide.region_3.4_spmd, body=%wide.region_1.3_spmd.sunk | while | flops 135267616 | bytes 12588135 | solution.py:49
  137.5 3.3 gather_fusion
  142.5 6.2 scatter_fusion
  148.9 3.3 gather_fusion
  152.2 1.7 fusion.37
  154.0 6.1 scatter_fusion
  160.2 3.3 gather_fusion
  165.3 6.1 scatter_fusion
  171.5 3.3 gather_fusion
  176.6 6.1 scatter_fusion
  185.2 3.6 fusion.21
  188.9 154.4 %reduce-scatter.2.cloned.1.call-done = f32[3072,128]{1,0:T(8,128)} async-done(((f32[3072,512]{1,0:T(8,128)}), f32[3072,128]{1,0:T(8,128)}) %reduce-scatter.2.cloned.1.call-update) | async-done | bytes 1572880 | tf_op jit(solution)/shard_map/reduce_scatter | solution.py:54
  343.3 3.3 multiply_convert_fusion
  346.8 34.9 %all-gather.2.cloned.1.call-done = bf16[3072,512]{1,0:T(8,128)(2,1)} async-done(((bf16[3072,128]{1,0:T(8,128)(2,1)}), bf16[3072,512]{1,0:T(8,128)(2,1)}) %all-gather.2.cloned.1.call-update) | async-done | bytes 3145744 | tf_op jit(solution)/shard_map/all_gather | solution.py:60
  381.7 3.8 convolution_convert_fusion
  385.5 5.6 broadcast_in_dim.57
  391.0 40.5 %while.21 = (s32[]{:T(128)}, f32[168,128,128]{2,1,0:T(8,128)}, s32[]{:T(128)}, s32[384]{0:T(512)S(1)}, bf16[384,128,128]{2,1,0:T(8,128)(2,1)}, /*index=5*/s32[38...) while((s32[]{:T(128)}, f32[168,128,128]{2,1,0:T(8,128)}, ...), condition=%wide.region_7.8_spmd, body=%wide.region_5.7_spmd.sunk | while | flops 135267648 | bytes 12588135 | solution.py:79
  391.2 1.9 gather_fusion.1
  393.1 1.8 fusion.40
  394.9 6.2 scatter_fusion.1
  401.3 1.9 gather_fusion.1
  403.2 1.8 fusion.40
  405.0 6.3 scatter_fusion.1
  411.5 1.9 gather_fusion.1
  413.4 1.8 fusion.40
  415.2 6.3 scatter_fusion.1
  421.6 1.9 gather_fusion.1
  423.5 1.8 fusion.40
  425.3 6.2 scatter_fusion.1
  431.5 6.4 fusion.20
  437.9 29.5 %collective-permute-start.6 = (f32[24,128,128]{2,1,0:T(8,128)S(1)}, f32[24,128,128]{2,1,0:T(8,128)S(1)}, u32[]{:S(2)}, u32[]{:S(2)}) collective-permute-start(f32[24,128,128]{2,1,0:T(8,128)S(1)} %get-tuple-element.129), channel_id=1, source_target_pairs={{0,244},{4,248},{8,252},{12,0},{16,4},{20,8},{24,12},{28,16},{32,2... | collective-permute-start | bytes 4718600 | tf_op jit(solution)/shard_map/ppermute | solution.py:17
  468.2 6.2 collective-permute-start.8
  474.4 92.2 %collective-permute-done.6 = f32[24,128,128]{2,1,0:T(8,128)S(1)} collective-permute-done((f32[24,128,128]{2,1,0:T(8,128)S(1)}, f32[24,128,128]{2,1,0:T(8,128)S(1)}, u32[]{:S(2)}, u32[]{:S(2)}) %collective-permute-start.6) | collective-permute-done | bytes 1572896 | tf_op jit(solution)/shard_map/ppermute | solution.py:17
  566.6 4.5 collective-permute-start.7
  572.5 596.9 %all-reduce.2.cloned.1.call-done = f32[128,512]{1,0:T(8,128)} async-done(((f32[128,512]{1,0:T(8,128)}), f32[128,512]{1,0:T(8,128)}) %all-reduce.2.cloned.1.call-update) | async-done | bytes 262160 | tf_op jit(solution)/shard_map/psum | solution.py:64
  1171.1 5.4 add_convert_fusion
  1176.5 9.2 scatter_custom_fusion.2
  (81 shorter events, 21.2 us)
Async XLA Ops:
  7.2 1.2 copy-start
  7.2 336.1 %reduce-scatter.2.cloned.1.call-start = ((), (), s32[]{:S(2)}) async-start(), calls=%async_computation.1 | async-start | bytes 7864320 | tf_op jit(solution)/shard_map/reduce_scatter | solution.py:54
  8.3 26.4 %copy-start.10 = (s32[384]{0:T(512)S(1)}, s32[384]{0:T(512)}, u32[]{:S(2)}) copy-start(s32[384]{0:T(512)} %param.14) | copy-start | bytes 4612
  8.3 26.4 %copy-start.9 = (s32[384]{0:T(512)S(1)}, s32[384]{0:T(512)}, u32[]{:S(2)}) copy-start(s32[384]{0:T(512)} %param.13) | copy-start | bytes 4612
  19.8 61.6 %collective-permute-start = (bf16[3072,128]{1,0:T(8,128)(2,1)}, bf16[3072,128]{1,0:T(8,128)(2,1)}, u32[]{:S(2)}, u32[]{:S(2)}) collective-permute-start(bf16[3072,128]{1,0:T(8,128)(2,1)} %broadcast_select_fusion), channel_id=1, source_target_pairs={{0,12},{4,16},{8,20},{12,24},{16,28},{20,32},{24,36},{28,40},{32,4... | collective-permute-start | bytes 2359304 | tf_op jit(solution)/shard_map/ppermute | solution.py:17
  24.4 87.7 %collective-permute-start.1 = (bf16[3072,128]{1,0:T(8,128)(2,1)}, bf16[3072,128]{1,0:T(8,128)(2,1)S(1)}, u32[]{:S(2)}, u32[]{:S(2)}) collective-permute-start(bf16[3072,128]{1,0:T(8,128)(2,1)} %broadcast_select_fusion), channel_id=1, source_target_pairs={{0,8},{4,12},{8,16},{12,20},{16,24},{20,28},{24,32},{28,36},{32,40... | collective-permute-start | bytes 2359304 | tf_op jit(solution)/shard_map/ppermute | solution.py:17
  28.0 106.2 %collective-permute-start.5 = (bf16[3072,128]{1,0:T(8,128)(2,1)}, bf16[3072,128]{1,0:T(8,128)(2,1)S(1)}, u32[]{:S(2)}, u32[]{:S(2)}) collective-permute-start(bf16[3072,128]{1,0:T(8,128)(2,1)} %broadcast_select_fusion), channel_id=1, source_target_pairs={{0,244},{4,248},{8,252},{12,0},{16,4},{20,8},{24,12},{28,16},{32,2... | collective-permute-start | bytes 2359304 | tf_op jit(solution)/shard_map/ppermute | solution.py:17
  31.1 103.0 %collective-permute-start.4 = (bf16[3072,128]{1,0:T(8,128)(2,1)}, bf16[3072,128]{1,0:T(8,128)(2,1)S(1)}, u32[]{:S(2)}, u32[]{:S(2)}) collective-permute-start(bf16[3072,128]{1,0:T(8,128)(2,1)} %broadcast_select_fusion), channel_id=1, source_target_pairs={{0,248},{4,252},{8,0},{12,4},{16,8},{20,12},{24,16},{28,20},{32,24... | collective-permute-start | bytes 2359304 | tf_op jit(solution)/shard_map/ppermute | solution.py:17
  34.1 96.8 %collective-permute-start.2 = (bf16[3072,128]{1,0:T(8,128)(2,1)}, bf16[3072,128]{1,0:T(8,128)(2,1)}, u32[]{:S(2)}, u32[]{:S(2)}) collective-permute-start(bf16[3072,128]{1,0:T(8,128)(2,1)} %broadcast_select_fusion), channel_id=1, source_target_pairs={{0,4},{4,8},{8,12},{12,16},{16,20},{20,24},{24,28},{28,32},{32,36}... | collective-permute-start | bytes 2359304 | tf_op jit(solution)/shard_map/ppermute | solution.py:17
  81.4 52.6 %collective-permute-start.3 = (bf16[3072,128]{1,0:T(8,128)(2,1)}, bf16[3072,128]{1,0:T(8,128)(2,1)S(1)}, u32[]{:S(2)}, u32[]{:S(2)}) collective-permute-start(bf16[3072,128]{1,0:T(8,128)(2,1)} %broadcast_select_fusion), channel_id=1, source_target_pairs={{0,252},{4,0},{8,4},{12,8},{16,12},{20,16},{24,20},{28,24},{32,28}... | collective-permute-start | bytes 2359304 | tf_op jit(solution)/shard_map/ppermute | solution.py:17
  134.4 2.9 copy-start.5
  137.3 47.9 %copy-start.8 = (bf16[128,512]{1,0:T(8,128)(2,1)S(1)}, bf16[128,512]{1,0:T(8,128)(2,1)}, u32[]{:S(2)}) copy-start(bf16[128,512]{1,0:T(8,128)(2,1)} %param.16) | copy-start | bytes 393220
  184.3 0.9 copy-start.3
  188.8 154.5 %copy-start.7 = (bf16[3072,128]{1,0:T(8,128)(2,1)S(1)}, bf16[3072,128]{1,0:T(8,128)(2,1)}, u32[]{:S(2)}) copy-start(bf16[3072,128]{1,0:T(8,128)(2,1)} %param.17) | copy-start | bytes 2359300
  188.8 192.9 %all-gather.2.cloned.1.call-start = ((), (), s32[]{:S(2)}) async-start(), calls=%async_computation.2 | async-start | bytes 3932160 | tf_op jit(solution)/shard_map/all_gather | solution.py:60
  346.6 822.8 %all-reduce.2.cloned.1.call-start = ((), (), s32[]{:S(2)}) async-start(), calls=%async_computation.3 | async-start | bytes 524288 | tf_op jit(solution)/shard_map/psum | solution.py:64
  431.5 139.6 %copy-start.2 = (bf16[3072,512]{1,0:T(8,128)(2,1)S(1)}, bf16[3072,512]{1,0:T(8,128)(2,1)}, u32[]{:S(2)}) copy-start(bf16[3072,512]{1,0:T(8,128)(2,1)} %all-gather.2.cloned.1.call-done) | copy-start | bytes 9437188
  431.5 139.6 %copy-start.4 = (bf16[24,128,128]{2,1,0:T(8,128)(2,1)S(1)}, bf16[24,128,128]{2,1,0:T(8,128)(2,1)}, u32[]{:S(2)}) copy-start(bf16[24,128,128]{2,1,0:T(8,128)(2,1)} %copy-done.3) | copy-start | bytes 2359300
  437.9 128.7 %collective-permute-start.6 = (f32[24,128,128]{2,1,0:T(8,128)S(1)}, f32[24,128,128]{2,1,0:T(8,128)S(1)}, u32[]{:S(2)}, u32[]{:S(2)}) collective-permute-start(f32[24,128,128]{2,1,0:T(8,128)S(1)} %get-tuple-element.129), channel_id=1, source_target_pairs={{0,244},{4,248},{8,252},{12,0},{16,4},{20,8},{24,12},{28,16},{32,2... | collective-permute-start | bytes 4718600 | tf_op jit(solution)/shard_map/ppermute | solution.py:17
  467.5 703.6 %collective-permute-start.11 = (f32[24,128,128]{2,1,0:T(8,128)}, f32[24,128,128]{2,1,0:T(8,128)}, u32[]{:S(2)}, u32[]{:S(2)}) collective-permute-start(f32[24,128,128]{2,1,0:T(8,128)} %get-tuple-element.130), channel_id=1, source_target_pairs={{0,12},{4,16},{8,20},{12,24},{16,28},{20,32},{24,36},{28,40},{32,4... | collective-permute-start | bytes 4718600 | tf_op jit(solution)/shard_map/ppermute | solution.py:17
  467.5 703.6 %collective-permute-start.10 = (f32[24,128,128]{2,1,0:T(8,128)}, f32[24,128,128]{2,1,0:T(8,128)}, u32[]{:S(2)}, u32[]{:S(2)}) collective-permute-start(f32[24,128,128]{2,1,0:T(8,128)} %get-tuple-element.131), channel_id=1, source_target_pairs={{0,8},{4,12},{8,16},{12,20},{16,24},{20,28},{24,32},{28,36},{32,40... | collective-permute-start | bytes 4718600 | tf_op jit(solution)/shard_map/ppermute | solution.py:17
  468.2 702.9 %collective-permute-start.9 = (f32[24,128,128]{2,1,0:T(8,128)}, f32[24,128,128]{2,1,0:T(8,128)}, u32[]{:S(2)}, u32[]{:S(2)}) collective-permute-start(f32[24,128,128]{2,1,0:T(8,128)} %get-tuple-element.132), channel_id=1, source_target_pairs={{0,4},{4,8},{8,12},{12,16},{16,20},{20,24},{24,28},{28,32},{32,36}... | collective-permute-start | bytes 4718600 | tf_op jit(solution)/shard_map/ppermute | solution.py:17
  468.2 702.9 %collective-permute-start.8 = (f32[24,128,128]{2,1,0:T(8,128)S(1)}, f32[24,128,128]{2,1,0:T(8,128)}, u32[]{:S(2)}, u32[]{:S(2)}) collective-permute-start(f32[24,128,128]{2,1,0:T(8,128)S(1)} %get-tuple-element.133), channel_id=1, source_target_pairs={{0,252},{4,0},{8,4},{12,8},{16,12},{20,16},{24,20},{28,24},{32,28}... | collective-permute-start | bytes 4718600 | tf_op jit(solution)/shard_map/ppermute | solution.py:17
  566.6 4.5 copy-start.6
  566.6 604.5 %collective-permute-start.7 = (f32[24,128,128]{2,1,0:T(8,128)S(1)}, f32[24,128,128]{2,1,0:T(8,128)}, u32[]{:S(2)}, u32[]{:S(2)}) collective-permute-start(f32[24,128,128]{2,1,0:T(8,128)S(1)} %get-tuple-element.134), channel_id=1, source_target_pairs={{0,248},{4,252},{8,0},{12,4},{16,8},{20,12},{24,16},{28,20},{32,24... | collective-permute-start | bytes 4718600 | tf_op jit(solution)/shard_map/ppermute | solution.py:17
  1171.1 14.6 %copy-start.1 = (bf16[3072,128]{1,0:T(8,128)(2,1)S(1)}, bf16[3072,128]{1,0:T(8,128)(2,1)}, u32[]{:S(2)}) copy-start(bf16[3072,128]{1,0:T(8,128)(2,1)} %param.11) | copy-start | bytes 2359300
Sparse Core Ops, SparseCore 0:
  189.0 154.2 reduce-scatter.1
  346.7 34.9 all-gather.1
  572.6 596.7 all-reduce.1
where the time goes:
time: 1200 us; the launch traced here: 1190 us
  waiting for transfers between devices  969 us (81%)
  other arithmetic  66.9 us (6%)
  local copies, waits for them, and re-layouts  59.7 us (5%)
  starting transfers between devices  59 us (5%)
  matrix products  22.8 us (2%)
  between operations  14.6 us (1%)
    psum x1, waiting for transfers between devices, body(): lax.psum(weight_terms, 'vertex') * (1.0 / math.sqrt(rows * devices))  597 us
    ppermute x12, waiting for transfers between devices, from_behind(): return lax.ppermute(value, axis, pairs)  183 us
    reduce_scatter x1, waiting for transfers between devices, body(): mixed = lax.psum_scatter(terms, 'feat', scatter_dimension=1, tiled=True)  154 us
    ppermute x12, starting transfers between devices, from_behind(): return lax.ppermute(value, axis, pairs)  58.7 us
    all_gather x1, waiting for transfers between devices, body(): grad_full = lax.all_gather(grad_mixed, 'feat', axis=1, tiled=True)  34.9 us
    scatter-add x4, other arithmetic, backward_step(): return partial_value.at[win_g].add(contrib)  25 us
    scatter-add x4, other arithmetic, forward_step(): return total.at[row_g].add(product)  24.5 us
  transfers between devices with their start and end apart: 15, of which 7 were waited for; matrix products, arithmetic and copies ran while one was open for 1% of the time, Pallas kernels for 0%

commit v1 on v0

v1 whole, which is shorter than its diff:
```python
import functools, math
import jax, jax.numpy as jnp
from jax import lax
from jax.experimental import pallas as pl
from jax.experimental.pallas import tpu as pltpu
from jax.sharding import PartitionSpec as P

REACH = 3
PARTS = 1
ROW_PARTS = 2
GROUPS = (2 * REACH + 1) * PARTS
wide_step = 8
narrow_step = 2
ring = 32
row_bits = 5
col_bits = 5

f32 = jnp.float32
bf16 = jnp.bfloat16
SMEM = pl.BlockSpec(memory_space=pltpu.SMEM)
VMEM = pl.BlockSpec(memory_space=pltpu.VMEM)
HBM = pl.BlockSpec(memory_space=pltpu.HBM)


def near(*values):
    return [pltpu.with_memory_space_constraint(v, pltpu.VMEM) for v in values]


def group_of(offset):
    return 2 * abs(offset) - (1 if offset < 0 else 0)


def keys(*reaches):
    return [group_of(way * r) * PARTS + p for r in reaches for way in ((-1, 1) if r else (1,)) for p in range(PARTS)]


def slot_plan(tile_row, tile_col, here, blocks, devices):
    slots = tile_row.shape[0]
    owner = tile_col // blocks
    local = tile_col - owner * blocks
    span = blocks // PARTS
    part = local // span
    offset = (owner - here + devices + REACH) % devices - REACH
    even_side = (offset > 0) == (here % 2 == 0)
    group = (2 * jnp.abs(offset) - (even_side & (offset != 0)).astype(jnp.int32)) * PARTS + part
    group = jnp.where(tile_row < blocks, group, GROUPS)
    slot = jnp.arange(slots, dtype=jnp.int32)
    packed = (slot << (row_bits + col_bits)) | (tile_row << col_bits) | (local - part * span)
    same = (group[:, None] == group[None, :]) & (slot[None, :] < slot[:, None])
    rank = jnp.sum(same.astype(jnp.int32), axis=1)
    ids = jnp.arange(GROUPS, dtype=jnp.int32)
    counts = jnp.sum((group[:, None] == ids[None, :]).astype(jnp.int32), axis=0)
    steps = (counts + narrow_step - 1) // narrow_step * narrow_step
    ends = jnp.sum(jnp.where(ids[:, None] >= ids[None, :], steps[None, :], 0), axis=1)
    starts = ends - steps
    base = jnp.sum(jnp.where(group[:, None] == ids[None, :], starts[None, :], 0), axis=1)
    place = jnp.where(group < GROUPS, base + rank, -1)
    places = slots + GROUPS * narrow_step
    dummy = blocks << col_bits
    index = jnp.arange(places, dtype=jnp.int32)
    plan = dummy + jnp.sum(
        jnp.where(index[:, None] == place[None, :], packed[None, :] - dummy, 0), axis=1
    )
    return plan, jnp.concatenate([starts, ends])


def each_slot(plan, spans, tiles, buffer, sems, groups, use):
    low, high = spans[groups[0]], spans[GROUPS + groups[-1]]

    def copy(k):
        at = k & (ring - 1)
        return pltpu.make_async_copy(tiles.at[plan[k] >> (row_bits + col_bits)], buffer.at[at], sems.at[at])

    def prime(k, carry):
        copy(k).start()
        return carry

    lax.fori_loop(low, jnp.minimum(high, low + ring), prime, 0)
    for i, group in enumerate(groups):
        start, end = spans[group], spans[GROUPS + group]

        def step(k, size, i=i):
            for j in range(size):
                copy(k + j).wait()
            use(i, [plan[k + j] for j in range(size)], [buffer.at[(k + j) & (ring - 1)] for j in range(size)])

            @pl.when(k + size + ring <= high)
            def _():
                for j in range(size):
                    copy(k + j + ring).start()

            if size > narrow_step:

                @pl.when(k + size + ring > high)
                def _():
                    lax.fori_loop(k + ring, jnp.minimum(k + size + ring, high), prime, 0)

        whole = lax.div(end - start, wide_step)
        middle = start + whole * wide_step

        @pl.loop(0, whole)
        def _(s):
            step(start + s * wide_step, wide_step)

        @pl.loop(0, lax.div(end - middle, narrow_step))
        def _(s):
            step(middle + s * narrow_step, narrow_step)


def forward_kernel(groups, first, last, plan, spans, tiles, *refs):
    windows = refs[: len(groups)]
    rest = refs[len(groups) :]
    if not first:
        total_in, rest = rest[0], rest[1:]
    outs, (total, buffer, sems) = rest[:-3], rest[-3:]
    side = buffer.shape[-1]
    blocks = total.shape[0] - 1
    if first:
        total[...] = jnp.zeros_like(total)
    else:
        total[:blocks] = total_in[...]

    def use(i, packed, tile):
        values = []
        for p, t in zip(packed, tile):
            col = p & ((1 << col_bits) - 1)
            source = windows[i][pl.ds(pl.multiple_of(col * side, side), side), :]
            values.append(jnp.dot(t[...], source, preferred_element_type=f32))
        for p, value in zip(packed, values):
            total[(p >> col_bits) & ((1 << row_bits) - 1)] += value

    each_slot(plan, spans, tiles, buffer, sems, groups, use)
    share = blocks // len(outs)
    for p, out in enumerate(outs):
        out[...] = total[p * share : (p + 1) * share].astype(out.dtype)


def forward_group(groups, first, last, plan, spans, tiles, windows, total):
    side = tiles.shape[-1]
    blocks = PARTS * windows[0].shape[0] // side
    shape = (blocks, side, windows[0].shape[1])
    return pl.pallas_call(
        functools.partial(forward_kernel, groups, first, last),
        out_shape=[pltpu.VMEM((blocks // ROW_PARTS, *shape[1:]), bf16)] * ROW_PARTS if last else [pltpu.VMEM(shape, f32)],
        in_specs=[SMEM, SMEM, HBM] + [VMEM] * (len(groups) + (not first)),
        out_specs=[VMEM] * (ROW_PARTS if last else 1),
        scratch_shapes=[
            pltpu.VMEM((blocks + 1, *shape[1:]), f32),
            pltpu.VMEM((ring, side, side), bf16),
            pltpu.SemaphoreType.DMA((ring,)),
        ],
        cost_estimate=pl.CostEstimate(
            flops=len(groups) * 30 * 2**22, bytes_accessed=len(groups) * 30 * 2**15, transcendentals=0
        ),
        compiler_params=pltpu.CompilerParams(vmem_limit_bytes=16 * 2**20),
        name="forward_group",
    )(plan, spans, tiles, *near(*windows, *([] if first else [total])))


def backward_kernel(groups, plan, spans, tiles, *refs):
    outs = refs[ROW_PARTS:-4]
    grad, total, buffer, sems = refs[-4:]
    blocks = grad.shape[0]
    share = blocks // ROW_PARTS
    for p in range(ROW_PARTS):
        grad[p * share : (p + 1) * share] = refs[p][...]
    span = blocks // PARTS
    total[...] = jnp.zeros_like(total)

    def use(i, packed, tile):
        values = []
        for p, t in zip(packed, tile):
            row = (p >> col_bits) & ((1 << row_bits) - 1)
            values.append(jnp.dot(grad[jnp.minimum(row, blocks - 1)], t[...], preferred_element_type=f32))
        for p, value in zip(packed, values):
            row = (p >> col_bits) & ((1 << row_bits) - 1)
            col = i * span + (p & ((1 << col_bits) - 1))
            total[jnp.where(row == blocks, total.shape[0] - 1, col)] += value

    each_slot(plan, spans, tiles, buffer, sems, groups, use)
    for o, out in enumerate(outs):
        out[...] = total[o * span : (o + 1) * span].astype(out.dtype)


def backward_group(groups, plan, spans, tiles, grads, dtypes):
    blocks, width, side = grads[0].shape
    blocks = blocks * ROW_PARTS
    shape = (blocks, width, side)
    part = (blocks // PARTS, width, side)
    return pl.pallas_call(
        functools.partial(backward_kernel, groups),
        out_shape=[pltpu.VMEM(part, d) for d in dtypes],
        in_specs=[SMEM, SMEM, HBM] + [VMEM] * ROW_PARTS,
        out_specs=[VMEM] * len(dtypes),
        scratch_shapes=[
            pltpu.VMEM(shape, bf16),
            pltpu.VMEM((len(dtypes) * part[0] + 1, width, side), f32),
            pltpu.VMEM((ring, side, side), bf16),
            pltpu.SemaphoreType.DMA((ring,)),
        ],
        cost_estimate=pl.CostEstimate(
            flops=len(groups) * 30 * 2**22, bytes_accessed=len(groups) * 30 * 2**15, transcendentals=0
        ),
        compiler_params=pltpu.CompilerParams(vmem_limit_bytes=16 * 2**20),
        name="backward_group",
    )(plan, spans, tiles, *near(*grads))


def swap(value, first):
    count = lax.axis_size("vertex")
    pairs = []
    for low in range(first, count + first, 2):
        pairs += [(low % count, (low + 1) % count), ((low + 1) % count, low % count)]
    return lax.ppermute(value, "vertex", pairs)


def exchange(value, step):
    count = lax.axis_size("feat")
    return lax.ppermute(value, "feat", [(source, source ^ step) for source in range(count)])


def gather_feat(value):
    far = exchange(value, 2)
    return [value, exchange(value, 1), far, exchange(far, 1)]


def gather_kernel(part, perm, base, source, out, wide, moved):
    rows = out.shape[0]
    wide[...] = source[...].astype(f32)
    first = base[0]

    @pl.loop(0, rows // 16)
    def _(step):
        at = step * 16
        for j in range(16):
            moved[pl.ds(at + j, 1), :] = wide[pl.ds(perm[part * rows + at + j] - first, 1), :]

    out[...] = moved[...].astype(out.dtype)


def gather_rows(part, perm, base, source):
    shape = (perm.shape[0] // PARTS, source.shape[1])
    return pl.pallas_call(
        functools.partial(gather_kernel, part),
        out_shape=pltpu.VMEM(shape, source.dtype),
        in_specs=[SMEM, SMEM, VMEM],
        out_specs=VMEM,
        scratch_shapes=[pltpu.VMEM(source.shape, f32), pltpu.VMEM(shape, f32)],
        cost_estimate=pl.CostEstimate(flops=0, bytes_accessed=12 * 2**20, transcendentals=0),
        compiler_params=pltpu.CompilerParams(vmem_limit_bytes=8 * 2**20),
        name="gather_rows",
    )(perm, base, source)


def mix_kernel(part, block_rows, shard, *refs):
    agg, cot, weight = refs[0:4], refs[4:8], refs[8:12]
    act, grad_agg, grad_weight, full, total = refs[-5:]
    rows, width = agg[1].shape
    columns = [pl.ds(pl.multiple_of((shard[0] ^ k) * width, width), width) for k in range(4)]
    for i in range(4):
        for k, c in enumerate(columns):
            full[i * width : (i + 1) * width, k * width : (k + 1) * width] = weight[i][:, c]
    total[...] = jnp.zeros_like(total)
    side = grad_agg.shape[2]

    @pl.loop(0, rows // block_rows)
    def _(step):
        here = pl.ds(pl.multiple_of(step * block_rows, block_rows), block_rows)
        whole = pl.ds(pl.multiple_of(part * rows + step * block_rows, block_rows), block_rows)
        mine = agg[0][here, :]
        mixed = jnp.dot(
            jnp.concatenate([a[here, :] for a in agg], axis=1), full[...], preferred_element_type=f32
        )
        sig = 0.5 + 0.5 * jnp.tanh(0.5 * mixed)
        cotangent = jnp.concatenate([c[whole, :] for c in cot], axis=1).astype(f32)
        grad = (cotangent * sig * (1.0 + mixed * (1.0 - sig))).astype(bf16)
        act[here, :] = (mixed[:, :width] * sig[:, :width]).astype(bf16)
        back = lax.dot_general(full[:width, :], grad, (((1,), (1,)), ((), ())), preferred_element_type=f32)
        for b in range(block_rows // side):
            grad_agg[step * (block_rows // side) + b] = back[:, b * side : (b + 1) * side].astype(bf16)
        total[...] += lax.dot_general(mine, grad, (((0,), (0,)), ((), ())), preferred_element_type=f32)

    for k in range(4):
        grad_weight[shard[0] ^ k] = total[:, k * width : (k + 1) * width]


def mix(part, shard, agg, cot, weight, side, block_rows):
    rows, width = agg[1].shape
    full = weight[0].shape[1]
    return pl.pallas_call(
        functools.partial(mix_kernel, part, block_rows),
        out_shape=[
            jax.ShapeDtypeStruct((rows, width), bf16),
            pltpu.VMEM((rows // side, width, side), bf16),
            pltpu.VMEM((full // width, width, width), f32),
        ],
        in_specs=[SMEM] + [VMEM] * 12,
        out_specs=[VMEM] * 3,
        scratch_shapes=[pltpu.VMEM((full, full), bf16), pltpu.VMEM((width, full), f32)],
        cost_estimate=pl.CostEstimate(
            flops=3 * rows * full * full, bytes_accessed=8 * rows * full, transcendentals=rows * full
        ),
        compiler_params=pltpu.CompilerParams(vmem_limit_bytes=16 * 2**20),
        name="mix",
    )(shard, *near(*agg, *cot), *weight)


def add_kernel(carried, own, out):
    out[...] = (carried[...].astype(f32) + own[...].astype(f32)).astype(bf16)


def add_part(carried, own):
    return pl.pallas_call(
        add_kernel,
        out_shape=pltpu.VMEM(carried.shape, bf16),
        in_specs=[VMEM] * 2,
        out_specs=VMEM,
        cost_estimate=pl.CostEstimate(flops=0, bytes_accessed=6 * carried.size, transcendentals=0),
        compiler_params=pltpu.CompilerParams(vmem_limit_bytes=4 * 2**20),
        name="add_part",
    )(*near(carried, own))


def scatter_kernel(perm, base, own, left, right, out, moved, wide):
    first = base[0]
    blocks, width, side = own.shape

    @pl.loop(0, blocks)
    def _(b):
        total = own[b] + left[b].astype(f32) + right[b].astype(f32)
        wide[...] = total.T
        at = b * side
        for j in range(side):
            moved[pl.ds(perm[at + j] - first, 1), :] = wide[j : j + 1, :]

    out[...] = moved[...].astype(out.dtype)


def scatter_rows(perm, base, own, left, right):
    width = own.shape[1]
    rows = perm.shape[0]
    return pl.pallas_call(
        scatter_kernel,
        out_shape=jax.ShapeDtypeStruct((rows, width), bf16),
        in_specs=[SMEM, SMEM] + [VMEM] * 3,
        out_specs=VMEM,
        scratch_shapes=[pltpu.VMEM((rows, width), f32), pltpu.VMEM((own.shape[2], width), f32)],
        cost_estimate=pl.CostEstimate(flops=0, bytes_accessed=12 * 2**20, transcendentals=0),
        compiler_params=pltpu.CompilerParams(vmem_limit_bytes=8 * 2**20),
        name="scatter_rows",
    )(perm, base, *near(own, left, right))


def sum_share(value):
    split = value.reshape(lax.axis_size("vertex"), -1, value.shape[-1])
    return jnp.sum(lax.all_to_all(split, "vertex", 0, 0, tiled=True), axis=0)


def spread_shares(mine, scale):
    spread = jnp.broadcast_to((mine * scale)[None], (lax.axis_size("vertex"), *mine.shape))
    return lax.all_to_all(spread, "vertex", 0, 0, tiled=True)


def body(features, tiles, tile_row, tile_col, permutation, weight, cotangent):
    rows, width = features.shape
    side = tiles.shape[1]
    blocks = rows // side
    devices = lax.axis_size("vertex")
    here = lax.axis_index("vertex")
    base = (here * rows).astype(jnp.int32).reshape(1)
    shard = lax.axis_index("feat").astype(jnp.int32).reshape(1)
    span = rows // ROW_PARTS
    scale = 1.0 / math.sqrt(rows * devices)
    tiles = pltpu.with_memory_space_constraint(tiles, pltpu.HBM)

    far = exchange(cotangent, 2)
    weight_far = exchange(weight, 2)
    ordered = gather_rows(0, permutation, base, features)
    plan, spans = slot_plan(tile_row, tile_col, here, blocks, devices)
    ordered, far, weight_far = lax.optimization_barrier((ordered, far, weight_far))

    even, odd = swap(ordered, 0), swap(ordered, 1)
    windows = [ordered, even, odd]
    weight_full = [weight, exchange(weight, 1), weight_far, exchange(weight_far, 1)]
    cot_full = [cotangent, exchange(cotangent, 1), far, exchange(far, 1)]
    for reach in range(2, REACH + 1):
        even, odd, plan = lax.optimization_barrier((even, odd, plan))
        even, odd = swap(odd, 0), swap(even, 1)
        windows += [even, odd]
    (total,) = forward_group(keys(*range(REACH)), True, False, plan, spans, tiles, windows[:-2], None)
    total, weight_full, cot_full = lax.optimization_barrier((total, weight_full, cot_full))
    total = forward_group(keys(REACH), False, True, plan, spans, tiles, windows[-2:], total)
    aggregated = [t.reshape(span, width) for t in total]

    acts, grads, terms = [], [], []
    for p in range(ROW_PARTS):
        act, grad, term = mix(p, shard, gather_feat(aggregated[p]), cot_full, weight_full, side, 2 * side)
        acts.append(act)
        grads.append(grad)
        terms.append(term)
    activations = jnp.concatenate(acts, axis=0)

    def after(token, value):
        return lax.optimization_barrier((exchange(token[0, :16], 1), value))[1]

    even, odd = backward_group(keys(REACH), plan, spans, tiles, grads, [bf16] * 2)
    share = sum_share(after(even, sum(terms)))
    even, odd = swap(even, 0), swap(odd, 1)
    own = backward_group(keys(2), plan, spans, tiles, grads, [bf16] * 2)
    even, odd, plan = lax.optimization_barrier((even, odd, plan))
    even, odd = add_part(odd, own[0]), add_part(even, own[1])
    even, odd = swap(even, 0), swap(odd, 1)
    own = backward_group(keys(0, 1), plan, spans, tiles, grads, [f32] + [bf16] * 2)
    even, odd = add_part(odd, own[1]), add_part(even, own[2])
    share = spread_shares(after(even, share), scale)
    even, odd = swap(even, 0), swap(odd, 1)
    even, odd, activations = lax.optimization_barrier((even, odd, activations))
    grad_features = scatter_rows(permutation, base, own[0], even, odd)
    share = share.reshape(-1, width, width)
    grad_weight = jnp.concatenate([share[k] for k in range(share.shape[0])], axis=1)
    return (activations, grad_features, grad_weight)


def solution(mesh):
    in_specs = (
        P("vertex", "feat"),
        P("vertex", None, None),
        P("vertex"),
        P("vertex"),
        P("vertex"),
        P("feat", None),
        P("vertex", "feat"),
    )
    out_specs = (P("vertex", "feat"), P("vertex", "feat"), P("feat", None))
    return jax.shard_map(body, mesh=mesh, in_specs=in_specs, out_specs=out_specs, check_vma=False)
```

time: 1200 us -> 219 us (0.18)
  waiting for transfers between devices: 969 us -> 96.3 us
  other arithmetic: 66.9 us -> 3.31 us
  Pallas kernels: 0 us -> 53.1 us
  local copies, waits for them, and re-layouts: 59.7 us -> 8.06 us
  matrix products: 22.8 us -> 0 us
  between operations: 14.6 us -> 0.9 us
    psum x1 -> x0, waiting for transfers between devices: 597 us -> none  [body(): lax.psum(weight_terms, 'vertex') * (1.0 / math.sqrt(rows * devices))]
    reduce_scatter x1 -> x0, waiting for transfers between devices: 154 us -> none  [body(): mixed = lax.psum_scatter(terms, 'feat', scatter_dimension=1, tiled=True)]
    ppermute x12 -> x24, waiting for transfers between devices: 183 us -> 96.3 us  [the longest x12 69.6 us: swap(): return lax.ppermute(value, 'vertex', pairs)]
    pallas_call x0 -> x13, Pallas kernels: none -> 53.1 us  [the longest x3 13.8 us: backward_group(): pl.pallas_call(functools.partial(backward_kernel, groups), out_shape=[plt...]
    scatter-add x8 -> x0, other arithmetic: 49.5 us -> none  [the longest x4 25 us: backward_step(): return partial_value.at[win_g].add(contrib)]
    all_gather x1 -> x0, waiting for transfers between devices: 34.9 us -> none  [body(): grad_full = lax.all_gather(grad_mixed, 'feat', axis=1, tiled=True)]
    gather x9 -> x0, local copies, waits for them, and re-layouts: 29.9 us -> none  [the longest x4 13.2 us: forward_step(): source = jnp.take(window_blocks, win_g, axis=0)]
    dot_general x11 -> x0, matrix products: 22.8 us -> none  [the longest x4 7.18 us: backward_step(): jnp.einsum('tji,tjf->tif', tile_g, source, preferred_element_type=jnp.flo...]
  transfers between devices with their start and end apart: 15 -> 26, of which waited for: 7 -> 15; matrix products, arithmetic and copies ran while one was open for 1% -> 2% of each run, Pallas kernels for 0% -> 15%
where the time goes in v1:
time: 219 us; the launch traced here: 218 us
  waiting for transfers between devices  96.3 us (44%)
  starting transfers between devices  56.3 us (26%)
  Pallas kernels  53.1 us (24%)
  local copies, waits for them, and re-layouts  8.06 us (4%)
  other arithmetic  3.31 us (2%)
    ppermute x12, waiting for transfers between devices, swap(): return lax.ppermute(value, 'vertex', pairs)  69.6 us
    ppermute x12, starting transfers between devices, swap(): return lax.ppermute(value, 'vertex', pairs)  37.6 us
    ppermute x12, waiting for transfers between devices, exchange(): lax.ppermute(value, 'feat', [(source, source ^ step) for source in range(...  26.8 us
    pallas_call x3, Pallas kernels, backward_group(): pl.pallas_call(functools.partial(backward_kernel, groups), out_shape=[plt...  13.8 us
    pallas_call x2, Pallas kernels, forward_group(): pl.pallas_call(functools.partial(forward_kernel, groups, first, last), ou...  11.1 us
    pallas_call x2, Pallas kernels, mix(): pl.pallas_call(functools.partial(mix_kernel, part, block_rows), out_shape...  10.8 us
    ppermute x12, starting transfers between devices, exchange(): lax.ppermute(value, 'feat', [(source, source ^ step) for source in range(...  8.41 us
    unnamed x34, local copies, waits for them, and re-layouts  7.32 us
  transfers between devices with their start and end apart: 26, of which 15 were waited for; matrix products, arithmetic and copies ran while one was open for 2% of the time, Pallas kernels for 15%

profile of v1, /device:TPU:16, one launch (start us, length us, event | category | flops | bytes accessed | tf_op | source)
XLA Modules:
  0.0 218.1 jit_solution(16300281931277014025)
XLA Ops:
  0.6 2.2 collective-permute-start
  2.8 1.5 collective-permute-start.1
  4.3 1.1 copy-done.3
  6.1 5.1 %gather_rows.1.refs_0_ = bf16[3072,128]{1,0:T(8,128)(2,1)S(1)} custom-call(s32[3072]{0:T(1024)S(1)} %copy-done.13, s32[1]{0:T(128)} %bitcast.base, bf16[3072,128]{1,0:T(8,128)(2,1)S(1)} %copy-done.3), custom_call_target="tpu_custom_call" | custom-call | bytes 12582912 | tf_op jit(solution)/shard_map/gather_rows/pallas_call | solution.py:243
  11.5 13.0 %collective-permute-done.1.refs_10_ = bf16[128,512]{1,0:T(8,128)(2,1)S(1)} collective-permute-done((bf16[128,512]{1,0:T(8,128)(2,1)}, bf16[128,512]{1,0:T(8,128)(2,1)S(1)}, u32[]{:S(2)}, u32[]{:S(2)}) %collective-permute-start.1) | collective-permute-done | bytes 131104 | tf_op jit(solution)/shard_map/ppermute | solution.py:219
  24.5 1.9 collective-permute-start.2
  26.5 7.9 %collective-permute-start.3 = (bf16[3072,128]{1,0:T(8,128)(2,1)S(1)}, bf16[3072,128]{1,0:T(8,128)(2,1)S(1)}, u32[]{:S(2)}, u32[]{:S(2)}) collective-permute-start(bf16[3072,128]{1,0:T(8,128)(2,1)S(1)} %gather_rows.1.refs_0_), channel_id=1, source_target_pairs={{4,8},{8,4},{12,16},{16,12},{20,24},{24,20},{28,32},{32,28},{36,40... | collective-permute-start | bytes 2359304 | tf_op jit(solution)/shard_map/ppermute | solution.py:214
  34.8 8.3 %collective-permute-done.2.refs_1_ = bf16[3072,128]{1,0:T(8,128)(2,1)S(1)} collective-permute-done((bf16[3072,128]{1,0:T(8,128)(2,1)S(1)}, bf16[3072,128]{1,0:T(8,128)(2,1)S(1)}, u32[]{:S(2)}, u32[]{:S(2)}) %collective-permute-start.2) | collective-permute-done | bytes 786464 | tf_op jit(solution)/shard_map/ppermute | solution.py:214
  43.1 7.6 %collective-permute-done.3.refs_2_ = bf16[3072,128]{1,0:T(8,128)(2,1)S(1)} collective-permute-done((bf16[3072,128]{1,0:T(8,128)(2,1)S(1)}, bf16[3072,128]{1,0:T(8,128)(2,1)S(1)}, u32[]{:S(2)}, u32[]{:S(2)}) %collective-permute-start.3) | collective-permute-done | bytes 786464 | tf_op jit(solution)/shard_map/ppermute | solution.py:214
  50.7 6.0 %collective-permute-start.5 = (bf16[3072,128]{1,0:T(8,128)(2,1)S(1)}, bf16[3072,128]{1,0:T(8,128)(2,1)S(1)}, u32[]{:S(2)}, u32[]{:S(2)}) collective-permute-start(bf16[3072,128]{1,0:T(8,128)(2,1)S(1)} %collective-permute-done.2.refs_1_), channel_id=1, source_target_pairs={{4,8},{8,4},{12,16},{16,12},{20,24},{24,20},{28,32},{32,28},{36,40... | collective-permute-start | bytes 2359304 | tf_op jit(solution)/shard_map/ppermute | solution.py:214
  57.2 11.0 %collective-permute-done.4.refs_3_ = bf16[3072,128]{1,0:T(8,128)(2,1)S(1)} collective-permute-done((bf16[3072,128]{1,0:T(8,128)(2,1)S(1)}, bf16[3072,128]{1,0:T(8,128)(2,1)S(1)}, u32[]{:S(2)}, u32[]{:S(2)}) %collective-permute-start.4) | collective-permute-done | bytes 786464 | tf_op jit(solution)/shard_map/ppermute | solution.py:214
  68.2 4.2 %collective-permute-done.5.refs_4_ = bf16[3072,128]{1,0:T(8,128)(2,1)S(1)} collective-permute-done((bf16[3072,128]{1,0:T(8,128)(2,1)S(1)}, bf16[3072,128]{1,0:T(8,128)(2,1)S(1)}, u32[]{:S(2)}, u32[]{:S(2)}) %collective-permute-start.5) | collective-permute-done | bytes 786464 | tf_op jit(solution)/shard_map/ppermute | solution.py:214
  72.4 5.7 %collective-permute-start.7 = (bf16[3072,128]{1,0:T(8,128)(2,1)S(1)}, bf16[3072,128]{1,0:T(8,128)(2,1)S(1)}, u32[]{:S(2)}, u32[]{:S(2)}) collective-permute-start(bf16[3072,128]{1,0:T(8,128)(2,1)S(1)} %collective-permute-done.4.refs_3_), channel_id=1, source_target_pairs={{4,8},{8,4},{12,16},{16,12},{20,24},{24,20},{28,32},{32,28},{36,40... | collective-permute-start | bytes 2359304 | tf_op jit(solution)/shard_map/ppermute | solution.py:214
  78.1 1.3 collective-permute-done.8.refs_9_
  79.7 6.8 %forward_group.2.refs_2_ = f32[24,128,128]{2,1,0:T(8,128)S(1)} custom-call(s32[398]{0:T(512)S(1)} %broadcast_add_fusion.plan, s32[14]{0:T(128)S(1)} %pad_add_fusion.spans, bf16[384,128,128]{2,1,0:T(8,128)(2,1)} %tiles.9, bf16[3072,128]{1,0:T(8,128)(2,1)S(1)} %gather_rows.1.refs_0_, bf16[3072,128]{1,0:T(8,128)(2,1)S(1)} %collective-permute-done.2.refs_1_, ...), custom_call_target="tpu_custom_call" | custom-call | flops 629145600 | bytes 4915200 | tf_op jit(solution)/shard_map/forward_group/pallas_call | solution.py:142
  86.6 0.9 copy-done.1
  87.4 1.5 collective-permute-done.6.refs_0_
  89.0 4.3 %collective-permute-done.7.refs_1_ = bf16[3072,128]{1,0:T(8,128)(2,1)S(1)} collective-permute-done((bf16[3072,128]{1,0:T(8,128)(2,1)S(1)}, bf16[3072,128]{1,0:T(8,128)(2,1)S(1)}, u32[]{:S(2)}, u32[]{:S(2)}) %collective-permute-start.7) | collective-permute-done | bytes 786464 | tf_op jit(solution)/shard_map/ppermute | solution.py:214
  93.3 4.3 %forward_group.3 = (bf16[12,128,128]{2,1,0:T(8,128)(2,1)}, bf16[12,128,128]{2,1,0:T(8,128)(2,1)S(1)}) custom-call(s32[398]{0:T(512)S(1)} %broadcast_add_fusion.plan, s32[14]{0:T(128)S(1)} %pad_add_fusion.spans, bf16[384,128,128]{2,1,0:T(8,128)(2,1)} %tiles.9, bf16[3072,128]{1,0:T(8,128)(2,1)S(1)} %collective-permute-done.6.refs_0_, ...), custom_call_target="tpu_custom_call" | custom-call | flops 251658240 | bytes 1966080 | tf_op jit(solution)/shard_map/forward_group/pallas_call | solution.py:142
  98.3 2.9 %collective-permute-start.13 = (bf16[1536,128]{1,0:T(8,128)(2,1)}, bf16[1536,128]{1,0:T(8,128)(2,1)}, u32[]{:S(2)}, u32[]{:S(2)}) collective-permute-start(bf16[1536,128]{1,0:T(8,128)(2,1)} %bitcast.2.refs_0_), channel_id=1, source_target_pairs={{0,2},{1,3},{2,0},{3,1},{4,6},{5,7},{6,4},{7,5},{8,10},{9,11},{10,... | collective-permute-start | bytes 1179656 | tf_op jit(solution)/shard_map/ppermute | solution.py:219
  101.2 0.8 copy-done.11
  102.0 8.6 %collective-permute-done.16.refs_2_ = bf16[1536,128]{1,0:T(8,128)(2,1)} collective-permute-done((bf16[1536,128]{1,0:T(8,128)(2,1)S(1)}, bf16[1536,128]{1,0:T(8,128)(2,1)}, u32[]{:S(2)}, u32[]{:S(2)}) %collective-permute-start.16) | collective-permute-done | bytes 393248 | tf_op jit(solution)/shard_map/ppermute | solution.py:219
  111.1 3.7 %collective-permute-done.13.refs_2_ = bf16[1536,128]{1,0:T(8,128)(2,1)} collective-permute-done((bf16[1536,128]{1,0:T(8,128)(2,1)}, bf16[1536,128]{1,0:T(8,128)(2,1)}, u32[]{:S(2)}, u32[]{:S(2)}) %collective-permute-start.13) | collective-permute-done | bytes 393248 | tf_op jit(solution)/shard_map/ppermute | solution.py:219
  114.8 1.1 copy-done.2
  116.0 1.0 copy-done.12
  117.0 5.3 %mix.3 = (bf16[1536,128]{1,0:T(8,128)(2,1)S(1)}, bf16[12,128,128]{2,1,0:T(8,128)(2,1)S(1)}, f32[4,128,128]{2,1,0:T(8,128)S(1)}) custom-call(s32[1]{0:T(128)} %bitcast.1.shard, bf16[1536,128]{1,0:T(8,128)(2,1)S(1)} %bitcast.15, bf16[1536,128]{1,0:T(8,128)(2,1)} %collective-permute-done.15.refs_1_, bf16[1536,128]{1,0:T(8,128)(2,1)} %collective-permute-done.16.refs_2_, ...), custom_call_target="tpu_custom_call" | custom-call | flops 1207959552 | bytes 6291456 | tf_op jit(solution)/shard_map/mix/pallas_call | solution.py:290
  123.0 1.0 copy-done.6
  124.0 5.4 %mix.2 = (bf16[1536,128]{1,0:T(8,128)(2,1)S(1)}, bf16[12,128,128]{2,1,0:T(8,128)(2,1)S(1)}, f32[4,128,128]{2,1,0:T(8,128)S(1)}) custom-call(s32[1]{0:T(128)} %bitcast.1.shard, bf16[1536,128]{1,0:T(8,128)(2,1)} %bitcast.2.refs_0_, bf16[1536,128]{1,0:T(8,128)(2,1)} %collective-permute-done.12.refs_1_, bf16[1536,128]{1,0:T(8,128)(2,1)} %collective-permute-done.13.refs_2_, ...), custom_call_target="tpu_custom_call" | custom-call | flops 1207959552 | bytes 6291456 | tf_op jit(solution)/shard_map/mix/pallas_call | solution.py:290
  129.5 4.6 %backward_group.3 = (bf16[24,128,128]{2,1,0:T(8,128)(2,1)}, bf16[24,128,128]{2,1,0:T(8,128)(2,1)S(1)}) custom-call(s32[398]{0:T(512)S(1)} %broadcast_add_fusion.plan, s32[14]{0:T(128)S(1)} %pad_add_fusion.spans, bf16[384,128,128]{2,1,0:T(8,128)(2,1)} %tiles.9, bf16[12,128,128]{2,1,0:T(8,128)(2,1)S(1)} %get-tuple-element.61.refs_0_, ...), custom_call_target="tpu_custom_call" | custom-call | flops 251658240 | bytes 1966080 | tf_op jit(solution)/shard_map/backward_group/pallas_call | solution.py:190
  134.2 4.7 %collective-permute-start.19 = (bf16[24,128,128]{2,1,0:T(8,128)(2,1)S(1)}, bf16[24,128,128]{2,1,0:T(8,128)(2,1)S(1)}, u32[]{:S(2)}, u32[]{:S(2)}) collective-permute-start(bf16[24,128,128]{2,1,0:T(8,128)(2,1)S(1)} %get-tuple-element.65), channel_id=1, source_target_pairs={{4,8},{8,4},{12,16},{16,12},{20,24},{24,20},{28,32},{32,28},{36,40... | collective-permute-start | bytes 2359304 | tf_op jit(solution)/shard_map/ppermute | solution.py:214
  138.9 0.7 add.70
  139.6 5.1 %all-to-all-start = ((f32[64,8,128]{2,1,0:T(8,128)}), f32[64,8,128]{2,1,0:T(8,128)S(1)}, u32[]{:S(2)}, u32[]{:S(2)}) async-start(f32[64,8,128]{2,1,0:T(8,128)} %bitcast.4), calls=%async_computation | async-start | bytes 524288 | tf_op jit(solution)/shard_map/all_to_all | solution.py:356
  144.7 3.8 %backward_group.4 = (bf16[24,128,128]{2,1,0:T(8,128)(2,1)S(1)}, bf16[24,128,128]{2,1,0:T(8,128)(2,1)S(1)}) custom-call(s32[398]{0:T(512)S(1)} %broadcast_add_fusion.plan, s32[14]{0:T(128)S(1)} %pad_add_fusion.spans, bf16[384,128,128]{2,1,0:T(8,128)(2,1)} %tiles.9, bf16[12,128,128]{2,1,0:T(8,128)(2,1)S(1)} %get-tuple-element.61.refs_0_, ...), custom_call_target="tpu_custom_call" | custom-call | flops 251658240 | bytes 1966080 | tf_op jit(solution)/shard_map/backward_group/pallas_call | solution.py:190
  148.5 7.6 %collective-permute-done.18.carried = bf16[24,128,128]{2,1,0:T(8,128)(2,1)S(1)} collective-permute-done((bf16[24,128,128]{2,1,0:T(8,128)(2,1)}, bf16[24,128,128]{2,1,0:T(8,128)(2,1)S(1)}, u32[]{:S(2)}, u32[]{:S(2)}) %collective-permute-start.18) | collective-permute-done | bytes 786464 | tf_op jit(solution)/shard_map/ppermute | solution.py:214
  156.1 6.5 %collective-permute-done.19.carried = bf16[24,128,128]{2,1,0:T(8,128)(2,1)S(1)} collective-permute-done((bf16[24,128,128]{2,1,0:T(8,128)(2,1)S(1)}, bf16[24,128,128]{2,1,0:T(8,128)(2,1)S(1)}, u32[]{:S(2)}, u32[]{:S(2)}) %collective-permute-start.19) | collective-permute-done | bytes 786464 | tf_op jit(solution)/shard_map/ppermute | solution.py:214
  162.6 1.1 add_part.6
  163.8 5.2 %collective-permute-start.20 = (bf16[24,128,128]{2,1,0:T(8,128)(2,1)S(1)}, bf16[24,128,128]{2,1,0:T(8,128)(2,1)}, u32[]{:S(2)}, u32[]{:S(2)}) collective-permute-start(bf16[24,128,128]{2,1,0:T(8,128)(2,1)S(1)} %add_part.4), channel_id=1, source_target_pairs={{4,8},{8,4},{12,16},{16,12},{20,24},{24,20},{28,32},{32,28},{36,40... | collective-permute-start | bytes 2359304 | tf_op jit(solution)/shard_map/ppermute | solution.py:214
  169.1 0.7 broadcast_in_dim.69
  169.9 5.2 %all-to-all-start.1 = ((f32[64,8,128]{2,1,0:T(8,128)}), f32[64,8,128]{2,1,0:T(8,128)S(1)}, u32[]{:S(2)}, u32[]{:S(2)}) async-start(f32[64,8,128]{2,1,0:T(8,128)} %broadcast_in_dim.69), calls=%async_computation.1 | async-start | bytes 524288 | tf_op jit(solution)/shard_map/all_to_all | solution.py:361
  175.1 5.4 %backward_group.5 = (f32[24,128,128]{2,1,0:T(8,128)S(1)}, bf16[24,128,128]{2,1,0:T(8,128)(2,1)S(1)}, bf16[24,128,128]{2,1,0:T(8,128)(2,1)S(1)}) custom-call(s32[398]{0:T(512)S(1)} %broadcast_add_fusion.plan, s32[14]{0:T(128)S(1)} %pad_add_fusion.spans, bf16[384,128,128]{2,1,0:T(8,128)(2,1)} %tiles.9, bf16[12,128,128]{2,1,0:T(8,128)(2,1)S(1)} %get-tuple-element.61.refs_0_, ...), custom_call_target="tpu_custom_call" | custom-call | flops 377487360 | bytes 2949120 | tf_op jit(solution)/shard_map/backward_group/pallas_call | solution.py:190
  180.5 4.1 %collective-permute-done.22.carried = bf16[24,128,128]{2,1,0:T(8,128)(2,1)} collective-permute-done((bf16[24,128,128]{2,1,0:T(8,128)(2,1)}, bf16[24,128,128]{2,1,0:T(8,128)(2,1)}, u32[]{:S(2)}, u32[]{:S(2)}) %collective-permute-start.22) | collective-permute-done | bytes 786464 | tf_op jit(solution)/shard_map/ppermute | solution.py:214
  184.6 2.2 %add_part.7 = bf16[24,128,128]{2,1,0:T(8,128)(2,1)} custom-call(bf16[24,128,128]{2,1,0:T(8,128)(2,1)} %collective-permute-done.22.carried, bf16[24,128,128]{2,1,0:T(8,128)(2,1)S(1)} %get-tuple-element.72.own), custom_call_target="tpu_custom_call" | custom-call | bytes 2359296 | tf_op jit(solution)/shard_map/add_part/pallas_call | solution.py:313
  186.8 6.1 %collective-permute-start.23 = (bf16[24,128,128]{2,1,0:T(8,128)(2,1)}, bf16[24,128,128]{2,1,0:T(8,128)(2,1)S(1)}, u32[]{:S(2)}, u32[]{:S(2)}) collective-permute-start(bf16[24,128,128]{2,1,0:T(8,128)(2,1)} %add_part.7), channel_id=1, source_target_pairs={{4,8},{8,4},{12,16},{16,12},{20,24},{24,20},{28,32},{32,28},{36,40... | collective-permute-start | bytes 2359304 | tf_op jit(solution)/shard_map/ppermute | solution.py:214
  192.9 2.2 %add_part.5 = bf16[24,128,128]{2,1,0:T(8,128)(2,1)} custom-call(bf16[24,128,128]{2,1,0:T(8,128)(2,1)} %collective-permute-done.20.carried, bf16[24,128,128]{2,1,0:T(8,128)(2,1)S(1)} %get-tuple-element.69.own), custom_call_target="tpu_custom_call" | custom-call | bytes 2359296 | tf_op jit(solution)/shard_map/add_part/pallas_call | solution.py:313
  195.2 0.9 pad_maximum_fusion
  196.8 12.3 %collective-permute-done.23.right = bf16[24,128,128]{2,1,0:T(8,128)(2,1)S(1)} collective-permute-done((bf16[24,128,128]{2,1,0:T(8,128)(2,1)}, bf16[24,128,128]{2,1,0:T(8,128)(2,1)S(1)}, u32[]{:S(2)}, u32[]{:S(2)}) %collective-permute-start.23) | collective-permute-done | bytes 786464 | tf_op jit(solution)/shard_map/ppermute | solution.py:214
  209.2 2.1 collective-permute-done.21.left
  211.3 6.8 %scatter_rows.1 = bf16[3072,128]{1,0:T(8,128)(2,1)} custom-call(s32[3072]{0:T(1024)S(1)} %copy-done.14, s32[1]{0:T(128)} %bitcast.base, f32[24,128,128]{2,1,0:T(8,128)S(1)} %get-tuple-element.76.own, bf16[24,128,128]{2,1,0:T(8,128)(2,1)S(1)} %collective-permute-done.21.left, bf16[24,128,128]{2,1,0:T(8,128)(2,1)S(1)} %collective-permute-done.23.right), custom_call_target="tpu_custom_call" | custom-call | bytes 12582912 | tf_op jit(solution)/shard_map/scatter_rows/pallas_call | solution.py:342
  (69 shorter events, 5.3 us)
Async XLA Ops:
  0.6 56.0 %copy-start = (bf16[3072,128]{1,0:T(8,128)(2,1)S(1)}, bf16[3072,128]{1,0:T(8,128)(2,1)}, u32[]{:S(2)}) copy-start(bf16[3072,128]{1,0:T(8,128)(2,1)} %refs_4_.1) | copy-start | bytes 2359300
  0.6 23.9 %collective-permute-start = (bf16[3072,128]{1,0:T(8,128)(2,1)}, bf16[3072,128]{1,0:T(8,128)(2,1)S(1)}, u32[]{:S(2)}, u32[]{:S(2)}) collective-permute-start(bf16[3072,128]{1,0:T(8,128)(2,1)} %refs_4_.1), channel_id=1, source_target_pairs={{0,2},{1,3},{2,0},{3,1},{4,6},{5,7},{6,4},{7,5},{8,10},{9,11},{10,... | collective-permute-start | bytes 2359304 | tf_op jit(solution)/shard_map/ppermute | solution.py:219
  2.8 21.7 %collective-permute-start.1 = (bf16[128,512]{1,0:T(8,128)(2,1)}, bf16[128,512]{1,0:T(8,128)(2,1)S(1)}, u32[]{:S(2)}, u32[]{:S(2)}) collective-permute-start(bf16[128,512]{1,0:T(8,128)(2,1)} %refs_8_.1), channel_id=1, source_target_pairs={{0,2},{1,3},{2,0},{3,1},{4,6},{5,7},{6,4},{7,5},{8,10},{9,11},{10,... | collective-permute-start | bytes 393224 | tf_op jit(solution)/shard_map/ppermute | solution.py:219
  4.3 1.1 copy-start.3
  5.4 0.7 copy-start.13
  6.1 5.1 %copy-start.15 = (s32[384]{0:T(512)S(1)}, s32[384]{0:T(512)}, u32[]{:S(2)}) copy-start(s32[384]{0:T(512)} %param.9) | copy-start | bytes 4612
  6.1 5.1 %copy-start.16 = (s32[384]{0:T(512)S(1)}, s32[384]{0:T(512)}, u32[]{:S(2)}) copy-start(s32[384]{0:T(512)} %param.10) | copy-start | bytes 4612
  6.1 72.0 %copy-start.4 = (bf16[128,512]{1,0:T(8,128)(2,1)S(1)}, bf16[128,512]{1,0:T(8,128)(2,1)}, u32[]{:S(2)}) copy-start(bf16[128,512]{1,0:T(8,128)(2,1)} %refs_8_.1) | copy-start | bytes 393220
  24.5 18.6 %collective-permute-start.2 = (bf16[3072,128]{1,0:T(8,128)(2,1)S(1)}, bf16[3072,128]{1,0:T(8,128)(2,1)S(1)}, u32[]{:S(2)}, u32[]{:S(2)}) collective-permute-start(bf16[3072,128]{1,0:T(8,128)(2,1)S(1)} %gather_rows.1.refs_0_), channel_id=1, source_target_pairs={{0,4},{4,0},{8,12},{12,8},{16,20},{20,16},{24,28},{28,24},{32,36},... | collective-permute-start | bytes 2359304 | tf_op jit(solution)/shard_map/ppermute | solution.py:214
  26.5 24.2 %collective-permute-start.3 = (bf16[3072,128]{1,0:T(8,128)(2,1)S(1)}, bf16[3072,128]{1,0:T(8,128)(2,1)S(1)}, u32[]{:S(2)}, u32[]{:S(2)}) collective-permute-start(bf16[3072,128]{1,0:T(8,128)(2,1)S(1)} %gather_rows.1.refs_0_), channel_id=1, source_target_pairs={{4,8},{8,4},{12,16},{16,12},{20,24},{24,20},{28,32},{32,28},{36,40... | collective-permute-start | bytes 2359304 | tf_op jit(solution)/shard_map/ppermute | solution.py:214
  50.7 17.5 %collective-permute-start.4 = (bf16[3072,128]{1,0:T(8,128)(2,1)S(1)}, bf16[3072,128]{1,0:T(8,128)(2,1)S(1)}, u32[]{:S(2)}, u32[]{:S(2)}) collective-permute-start(bf16[3072,128]{1,0:T(8,128)(2,1)S(1)} %collective-permute-done.3.refs_2_), channel_id=1, source_target_pairs={{0,4},{4,0},{8,12},{12,8},{16,20},{20,16},{24,28},{28,24},{32,36},... | collective-permute-start | bytes 2359304 | tf_op jit(solution)/shard_map/ppermute | solution.py:214
  50.7 21.7 %collective-permute-start.5 = (bf16[3072,128]{1,0:T(8,128)(2,1)S(1)}, bf16[3072,128]{1,0:T(8,128)(2,1)S(1)}, u32[]{:S(2)}, u32[]{:S(2)}) collective-permute-start(bf16[3072,128]{1,0:T(8,128)(2,1)S(1)} %collective-permute-done.2.refs_1_), channel_id=1, source_target_pairs={{4,8},{8,4},{12,16},{16,12},{20,24},{24,20},{28,32},{32,28},{36,40... | collective-permute-start | bytes 2359304 | tf_op jit(solution)/shard_map/ppermute | solution.py:214
  56.7 29.9 %collective-permute-start.10 = (bf16[3072,128]{1,0:T(8,128)(2,1)S(1)}, bf16[3072,128]{1,0:T(8,128)(2,1)S(1)}, u32[]{:S(2)}, u32[]{:S(2)}) collective-permute-start(bf16[3072,128]{1,0:T(8,128)(2,1)S(1)} %copy-done), channel_id=1, source_target_pairs={{0,1},{1,0},{2,3},{3,2},{4,5},{5,4},{6,7},{7,6},{8,9},{9,8},{10,11... | collective-permute-start | bytes 2359304 | tf_op jit(solution)/shard_map/ppermute | solution.py:219
  56.7 29.9 %collective-permute-start.11 = (bf16[3072,128]{1,0:T(8,128)(2,1)S(1)}, bf16[3072,128]{1,0:T(8,128)(2,1)S(1)}, u32[]{:S(2)}, u32[]{:S(2)}) collective-permute-start(bf16[3072,128]{1,0:T(8,128)(2,1)S(1)} %collective-permute-done.refs_6_), channel_id=1, source_target_pairs={{0,1},{1,0},{2,3},{3,2},{4,5},{5,4},{6,7},{7,6},{8,9},{9,8},{10,11... | collective-permute-start | bytes 2359304 | tf_op jit(solution)/shard_map/ppermute | solution.py:219
  72.4 16.6 %collective-permute-start.6 = (bf16[3072,128]{1,0:T(8,128)(2,1)S(1)}, bf16[3072,128]{1,0:T(8,128)(2,1)S(1)}, u32[]{:S(2)}, u32[]{:S(2)}) collective-permute-start(bf16[3072,128]{1,0:T(8,128)(2,1)S(1)} %collective-permute-done.5.refs_4_), channel_id=1, source_target_pairs={{0,4},{4,0},{8,12},{12,8},{16,20},{20,16},{24,28},{28,24},{32,36},... | collective-permute-start | bytes 2359304 | tf_op jit(solution)/shard_map/ppermute | solution.py:214
  72.4 20.9 %collective-permute-start.7 = (bf16[3072,128]{1,0:T(8,128)(2,1)S(1)}, bf16[3072,128]{1,0:T(8,128)(2,1)S(1)}, u32[]{:S(2)}, u32[]{:S(2)}) collective-permute-start(bf16[3072,128]{1,0:T(8,128)(2,1)S(1)} %collective-permute-done.4.refs_3_), channel_id=1, source_target_pairs={{4,8},{8,4},{12,16},{16,12},{20,24},{24,20},{28,32},{32,28},{36,40... | collective-permute-start | bytes 2359304 | tf_op jit(solution)/shard_map/ppermute | solution.py:214
  78.1 1.3 collective-permute-start.8
  79.5 7.1 %collective-permute-start.9 = (bf16[128,512]{1,0:T(8,128)(2,1)S(1)}, bf16[128,512]{1,0:T(8,128)(2,1)S(1)}, u32[]{:S(2)}, u32[]{:S(2)}) collective-permute-start(bf16[128,512]{1,0:T(8,128)(2,1)S(1)} %collective-permute-done.1.refs_10_), channel_id=1, source_target_pairs={{0,1},{1,0},{2,3},{3,2},{4,5},{5,4},{6,7},{7,6},{8,9},{9,8},{10,11... | collective-permute-start | bytes 393224 | tf_op jit(solution)/shard_map/ppermute | solution.py:219
  86.6 0.9 copy-start.1
  97.6 13.0 %collective-permute-start.16 = (bf16[1536,128]{1,0:T(8,128)(2,1)S(1)}, bf16[1536,128]{1,0:T(8,128)(2,1)}, u32[]{:S(2)}, u32[]{:S(2)}) collective-permute-start(bf16[1536,128]{1,0:T(8,128)(2,1)S(1)} %bitcast.13), channel_id=1, source_target_pairs={{0,2},{1,3},{2,0},{3,1},{4,6},{5,7},{6,4},{7,5},{8,10},{9,11},{10,... | collective-permute-start | bytes 1179656 | tf_op jit(solution)/shard_map/ppermute | solution.py:219
  98.3 16.5 %collective-permute-start.13 = (bf16[1536,128]{1,0:T(8,128)(2,1)}, bf16[1536,128]{1,0:T(8,128)(2,1)}, u32[]{:S(2)}, u32[]{:S(2)}) collective-permute-start(bf16[1536,128]{1,0:T(8,128)(2,1)} %bitcast.2.refs_0_), channel_id=1, source_target_pairs={{0,2},{1,3},{2,0},{3,1},{4,6},{5,7},{6,4},{7,5},{8,10},{9,11},{10,... | collective-permute-start | bytes 1179656 | tf_op jit(solution)/shard_map/ppermute | solution.py:219
  101.2 13.6 %collective-permute-start.15 = (bf16[1536,128]{1,0:T(8,128)(2,1)S(1)}, bf16[1536,128]{1,0:T(8,128)(2,1)}, u32[]{:S(2)}, u32[]{:S(2)}) collective-permute-start(bf16[1536,128]{1,0:T(8,128)(2,1)S(1)} %bitcast.14), channel_id=1, source_target_pairs={{0,1},{1,0},{2,3},{3,2},{4,5},{5,4},{6,7},{7,6},{8,9},{9,8},{10,11... | collective-permute-start | bytes 1179656 | tf_op jit(solution)/shard_map/ppermute | solution.py:219
  101.2 0.8 copy-start.11
  110.6 4.2 %collective-permute-start.17 = (bf16[1536,128]{1,0:T(8,128)(2,1)}, bf16[1536,128]{1,0:T(8,128)(2,1)}, u32[]{:S(2)}, u32[]{:S(2)}) collective-permute-start(bf16[1536,128]{1,0:T(8,128)(2,1)} %collective-permute-done.16.refs_2_), channel_id=1, source_target_pairs={{0,1},{1,0},{2,3},{3,2},{4,5},{5,4},{6,7},{7,6},{8,9},{9,8},{10,11... | collective-permute-start | bytes 1179656 | tf_op jit(solution)/shard_map/ppermute | solution.py:219
  110.6 12.3 %collective-permute-start.12 = (bf16[1536,128]{1,0:T(8,128)(2,1)}, bf16[1536,128]{1,0:T(8,128)(2,1)}, u32[]{:S(2)}, u32[]{:S(2)}) collective-permute-start(bf16[1536,128]{1,0:T(8,128)(2,1)} %bitcast.2.refs_0_), channel_id=1, source_target_pairs={{0,1},{1,0},{2,3},{3,2},{4,5},{5,4},{6,7},{7,6},{8,9},{9,8},{10,11... | collective-permute-start | bytes 1179656 | tf_op jit(solution)/shard_map/ppermute | solution.py:219
  114.8 8.1 %collective-permute-start.14 = (bf16[1536,128]{1,0:T(8,128)(2,1)}, bf16[1536,128]{1,0:T(8,128)(2,1)}, u32[]{:S(2)}, u32[]{:S(2)}) collective-permute-start(bf16[1536,128]{1,0:T(8,128)(2,1)} %collective-permute-done.13.refs_2_), channel_id=1, source_target_pairs={{0,1},{1,0},{2,3},{3,2},{4,5},{5,4},{6,7},{7,6},{8,9},{9,8},{10,11... | collective-permute-start | bytes 1179656 | tf_op jit(solution)/shard_map/ppermute | solution.py:219
  114.8 1.1 copy-start.2
  116.0 1.0 copy-start.12
  122.3 0.7 copy-start.5
  123.0 6.5 %copy-start.7 = (bf16[1536,128]{1,0:T(8,128)(2,1)}, bf16[1536,128]{1,0:T(8,128)(2,1)S(1)}, u32[]{:S(2)}) copy-start(bf16[1536,128]{1,0:T(8,128)(2,1)S(1)} %get-tuple-element.74) | copy-start | bytes 1179652
  123.0 1.0 copy-start.6
  129.5 4.6 %copy-start.9 = (bf16[1536,128]{1,0:T(8,128)(2,1)}, bf16[1536,128]{1,0:T(8,128)(2,1)S(1)}, u32[]{:S(2)}) copy-start(bf16[1536,128]{1,0:T(8,128)(2,1)S(1)} %get-tuple-element.73) | copy-start | bytes 1179652
  134.1 22.0 %collective-permute-start.18 = (bf16[24,128,128]{2,1,0:T(8,128)(2,1)}, bf16[24,128,128]{2,1,0:T(8,128)(2,1)S(1)}, u32[]{:S(2)}, u32[]{:S(2)}) collective-permute-start(bf16[24,128,128]{2,1,0:T(8,128)(2,1)} %get-tuple-element.64), channel_id=1, source_target_pairs={{0,4},{4,0},{8,12},{12,8},{16,20},{20,16},{24,28},{28,24},{32,36},... | collective-permute-start | bytes 2359304 | tf_op jit(solution)/shard_map/ppermute | solution.py:214
  134.2 28.4 %collective-permute-start.19 = (bf16[24,128,128]{2,1,0:T(8,128)(2,1)S(1)}, bf16[24,128,128]{2,1,0:T(8,128)(2,1)S(1)}, u32[]{:S(2)}, u32[]{:S(2)}) collective-permute-start(bf16[24,128,128]{2,1,0:T(8,128)(2,1)S(1)} %get-tuple-element.65), channel_id=1, source_target_pairs={{4,8},{8,4},{12,16},{16,12},{20,24},{24,20},{28,32},{32,28},{36,40... | collective-permute-start | bytes 2359304 | tf_op jit(solution)/shard_map/ppermute | solution.py:214
  139.6 29.5 %all-to-all-start = ((f32[64,8,128]{2,1,0:T(8,128)}), f32[64,8,128]{2,1,0:T(8,128)S(1)}, u32[]{:S(2)}, u32[]{:S(2)}) async-start(f32[64,8,128]{2,1,0:T(8,128)} %bitcast.4), calls=%async_computation | async-start | bytes 524288 | tf_op jit(solution)/shard_map/all_to_all | solution.py:356
  163.6 21.0 %collective-permute-start.22 = (bf16[24,128,128]{2,1,0:T(8,128)(2,1)}, bf16[24,128,128]{2,1,0:T(8,128)(2,1)}, u32[]{:S(2)}, u32[]{:S(2)}) collective-permute-start(bf16[24,128,128]{2,1,0:T(8,128)(2,1)} %add_part.6), channel_id=1, source_target_pairs={{0,4},{4,0},{8,12},{12,8},{16,20},{20,16},{24,28},{28,24},{32,36},... | collective-permute-start | bytes 2359304 | tf_op jit(solution)/shard_map/ppermute | solution.py:214
  163.8 29.1 %collective-permute-start.20 = (bf16[24,128,128]{2,1,0:T(8,128)(2,1)S(1)}, bf16[24,128,128]{2,1,0:T(8,128)(2,1)}, u32[]{:S(2)}, u32[]{:S(2)}) collective-permute-start(bf16[24,128,128]{2,1,0:T(8,128)(2,1)S(1)} %add_part.4), channel_id=1, source_target_pairs={{4,8},{8,4},{12,16},{16,12},{20,24},{24,20},{28,32},{32,28},{36,40... | collective-permute-start | bytes 2359304 | tf_op jit(solution)/shard_map/ppermute | solution.py:214
  169.9 26.2 %all-to-all-start.1 = ((f32[64,8,128]{2,1,0:T(8,128)}), f32[64,8,128]{2,1,0:T(8,128)S(1)}, u32[]{:S(2)}, u32[]{:S(2)}) async-start(f32[64,8,128]{2,1,0:T(8,128)} %broadcast_in_dim.69), calls=%async_computation.1 | async-start | bytes 524288 | tf_op jit(solution)/shard_map/all_to_all | solution.py:361
  186.8 8.3 %copy-start.8 = (bf16[1536,128]{1,0:T(8,128)(2,1)S(1)}, bf16[1536,128]{1,0:T(8,128)(2,1)}, u32[]{:S(2)}) copy-start(bf16[1536,128]{1,0:T(8,128)(2,1)} %copy-done.7) | copy-start | bytes 1179652
  186.8 8.3 %copy-start.10 = (bf16[1536,128]{1,0:T(8,128)(2,1)S(1)}, bf16[1536,128]{1,0:T(8,128)(2,1)}, u32[]{:S(2)}) copy-start(bf16[1536,128]{1,0:T(8,128)(2,1)} %copy-done.9) | copy-start | bytes 1179652
  186.8 22.4 %collective-permute-start.23 = (bf16[24,128,128]{2,1,0:T(8,128)(2,1)}, bf16[24,128,128]{2,1,0:T(8,128)(2,1)S(1)}, u32[]{:S(2)}, u32[]{:S(2)}) collective-permute-start(bf16[24,128,128]{2,1,0:T(8,128)(2,1)} %add_part.7), channel_id=1, source_target_pairs={{4,8},{8,4},{12,16},{16,12},{20,24},{24,20},{28,32},{32,28},{36,40... | collective-permute-start | bytes 2359304 | tf_op jit(solution)/shard_map/ppermute | solution.py:214
  195.1 16.2 %copy-start.14 = (s32[3072]{0:T(1024)S(1)}, s32[3072]{0:T(1024)}, u32[]{:S(2)}) copy-start(s32[3072]{0:T(1024)} %perm.3) | copy-start | bytes 36868
  195.1 16.2 %collective-permute-start.21 = (bf16[24,128,128]{2,1,0:T(8,128)(2,1)}, bf16[24,128,128]{2,1,0:T(8,128)(2,1)S(1)}, u32[]{:S(2)}, u32[]{:S(2)}) collective-permute-start(bf16[24,128,128]{2,1,0:T(8,128)(2,1)} %add_part.5), channel_id=1, source_target_pairs={{0,4},{4,0},{8,12},{12,8},{16,20},{20,16},{24,28},{28,24},{32,36},... | collective-permute-start | bytes 2359304 | tf_op jit(solution)/shard_map/ppermute | solution.py:214

commit v2 on v1

--- a/solution.py
+++ b/solution.py
@@ -394,7 +394,7 @@
 
     acts, grads, terms = [], [], []
     for p in range(ROW_PARTS):
-        act, grad, term = mix(p, shard, gather_feat(aggregated[p]), cot_full, weight_full, side, 2 * side)
+        act, grad, term = mix(p, shard, gather_feat(aggregated[p]), cot_full, weight_full, side, 6 * side)
         acts.append(act)
         grads.append(grad)
         terms.append(term)

time: 219 us -> 216 us (0.986)
  starting transfers between devices: 56.3 us -> 52.5 us
    ppermute x12, starting transfers between devices: 37.6 us -> 33.8 us  [swap(): return lax.ppermute(value, 'vertex', pairs)]
    pallas_call x2, Pallas kernels: 10.8 us -> 8.01 us  [mix(): pl.pallas_call(functools.partial(mix_kernel, part, block_rows), out_shape...]
  transfers between devices with their start and end apart: 26 -> 26, of which waited for: 15 -> 16; matrix products, arithmetic and copies ran while one was open for 2% -> 2% of each run, Pallas kernels for 15% -> 15%
where the time goes in v2:
time: 216 us; the launch traced here: 215 us
  waiting for transfers between devices  97.6 us (45%)
  Pallas kernels  52.7 us (24%)
  starting transfers between devices  52.5 us (24%)
  local copies, waits for them, and re-layouts  8.06 us (4%)
  other arithmetic  3.31 us (2%)
    ppermute x12, waiting for transfers between devices, swap(): return lax.ppermute(value, 'vertex', pairs)  70.9 us
    ppermute x12, starting transfers between devices, swap(): return lax.ppermute(value, 'vertex', pairs)  33.8 us
    ppermute x12, waiting for transfers between devices, exchange(): lax.ppermute(value, 'feat', [(source, source ^ step) for source in range(...  26.8 us
    pallas_call x3, Pallas kernels, backward_group(): pl.pallas_call(functools.partial(backward_kernel, groups), out_shape=[plt...  14.9 us
    pallas_call x2, Pallas kernels, forward_group(): pl.pallas_call(functools.partial(forward_kernel, groups, first, last), ou...  12.3 us
    ppermute x12, starting transfers between devices, exchange(): lax.ppermute(value, 'feat', [(source, source ^ step) for source in range(...  8.41 us
    pallas_call x2, Pallas kernels, mix(): pl.pallas_call(functools.partial(mix_kernel, part, block_rows), out_shape...  8.01 us
    unnamed x34, local copies, waits for them, and re-layouts  7.32 us
  transfers between devices with their start and end apart: 26, of which 16 were waited for; matrix products, arithmetic and copies ran while one was open for 2% of the time, Pallas kernels for 15%

profile of v2, /device:TPU:16, one launch (start us, length us, event | category | flops | bytes accessed | tf_op | source)
XLA Modules:
  0.0 215.1 jit_solution(15459911587965143108)
XLA Ops:
  0.6 2.2 %collective-permute-start = (bf16[3072,128]{1,0:T(8,128)(2,1)}, bf16[3072,128]{1,0:T(8,128)(2,1)S(1)}, u32[]{:S(2)}, u32[]{:S(2)}) collective-permute-start(bf16[3072,128]{1,0:T(8,128)(2,1)} %refs_4_.1), channel_id=1, source_target_pairs={{0,2},{1,3},{2,0},{3,1},{4,6},{5,7},{6,4},{7,5},{8,10},{9,11},{10,... | collective-permute-start | bytes 2359304 | tf_op jit(solution)/shard_map/ppermute | solution.py:219
  2.8 1.5 collective-permute-start.1
  4.3 1.1 copy-done.3
  6.1 5.1 %gather_rows.1.refs_0_ = bf16[3072,128]{1,0:T(8,128)(2,1)S(1)} custom-call(s32[3072]{0:T(1024)S(1)} %copy-done.13, s32[1]{0:T(128)} %bitcast.base, bf16[3072,128]{1,0:T(8,128)(2,1)S(1)} %copy-done.3), custom_call_target="tpu_custom_call" | custom-call | bytes 12582912 | tf_op jit(solution)/shard_map/gather_rows/pallas_call | solution.py:243
  11.5 13.0 %collective-permute-done.1.refs_10_ = bf16[128,512]{1,0:T(8,128)(2,1)S(1)} collective-permute-done((bf16[128,512]{1,0:T(8,128)(2,1)}, bf16[128,512]{1,0:T(8,128)(2,1)S(1)}, u32[]{:S(2)}, u32[]{:S(2)}) %collective-permute-start.1) | collective-permute-done | bytes 131104 | tf_op jit(solution)/shard_map/ppermute | solution.py:219
  24.5 1.9 collective-permute-start.2
  26.5 7.9 %collective-permute-start.3 = (bf16[3072,128]{1,0:T(8,128)(2,1)S(1)}, bf16[3072,128]{1,0:T(8,128)(2,1)S(1)}, u32[]{:S(2)}, u32[]{:S(2)}) collective-permute-start(bf16[3072,128]{1,0:T(8,128)(2,1)S(1)} %gather_rows.1.refs_0_), channel_id=1, source_target_pairs={{4,8},{8,4},{12,16},{16,12},{20,24},{24,20},{28,32},{32,28},{36,40... | collective-permute-start | bytes 2359304 | tf_op jit(solution)/shard_map/ppermute | solution.py:214
  34.8 8.3 %collective-permute-done.2.refs_1_ = bf16[3072,128]{1,0:T(8,128)(2,1)S(1)} collective-permute-done((bf16[3072,128]{1,0:T(8,128)(2,1)S(1)}, bf16[3072,128]{1,0:T(8,128)(2,1)S(1)}, u32[]{:S(2)}, u32[]{:S(2)}) %collective-permute-start.2) | collective-permute-done | bytes 786464 | tf_op jit(solution)/shard_map/ppermute | solution.py:214
  43.1 7.6 %collective-permute-done.3.refs_2_ = bf16[3072,128]{1,0:T(8,128)(2,1)S(1)} collective-permute-done((bf16[3072,128]{1,0:T(8,128)(2,1)S(1)}, bf16[3072,128]{1,0:T(8,128)(2,1)S(1)}, u32[]{:S(2)}, u32[]{:S(2)}) %collective-permute-start.3) | collective-permute-done | bytes 786464 | tf_op jit(solution)/shard_map/ppermute | solution.py:214
  50.7 6.0 %collective-permute-start.5 = (bf16[3072,128]{1,0:T(8,128)(2,1)S(1)}, bf16[3072,128]{1,0:T(8,128)(2,1)S(1)}, u32[]{:S(2)}, u32[]{:S(2)}) collective-permute-start(bf16[3072,128]{1,0:T(8,128)(2,1)S(1)} %collective-permute-done.2.refs_1_), channel_id=1, source_target_pairs={{4,8},{8,4},{12,16},{16,12},{20,24},{24,20},{28,32},{32,28},{36,40... | collective-permute-start | bytes 2359304 | tf_op jit(solution)/shard_map/ppermute | solution.py:214
  57.2 11.0 %collective-permute-done.4.refs_3_ = bf16[3072,128]{1,0:T(8,128)(2,1)S(1)} collective-permute-done((bf16[3072,128]{1,0:T(8,128)(2,1)S(1)}, bf16[3072,128]{1,0:T(8,128)(2,1)S(1)}, u32[]{:S(2)}, u32[]{:S(2)}) %collective-permute-start.4) | collective-permute-done | bytes 786464 | tf_op jit(solution)/shard_map/ppermute | solution.py:214
  68.2 4.2 %collective-permute-done.5.refs_4_ = bf16[3072,128]{1,0:T(8,128)(2,1)S(1)} collective-permute-done((bf16[3072,128]{1,0:T(8,128)(2,1)S(1)}, bf16[3072,128]{1,0:T(8,128)(2,1)S(1)}, u32[]{:S(2)}, u32[]{:S(2)}) %collective-permute-start.5) | collective-permute-done | bytes 786464 | tf_op jit(solution)/shard_map/ppermute | solution.py:214
  72.4 5.7 %collective-permute-start.7 = (bf16[3072,128]{1,0:T(8,128)(2,1)S(1)}, bf16[3072,128]{1,0:T(8,128)(2,1)S(1)}, u32[]{:S(2)}, u32[]{:S(2)}) collective-permute-start(bf16[3072,128]{1,0:T(8,128)(2,1)S(1)} %collective-permute-done.4.refs_3_), channel_id=1, source_target_pairs={{4,8},{8,4},{12,16},{16,12},{20,24},{24,20},{28,32},{32,28},{36,40... | collective-permute-start | bytes 2359304 | tf_op jit(solution)/shard_map/ppermute | solution.py:214
  78.1 1.3 collective-permute-done.8.refs_9_
  79.7 7.7 %forward_group.2.refs_2_ = f32[24,128,128]{2,1,0:T(8,128)S(1)} custom-call(s32[398]{0:T(512)S(1)} %broadcast_add_fusion.plan, s32[14]{0:T(128)S(1)} %pad_add_fusion.spans, bf16[384,128,128]{2,1,0:T(8,128)(2,1)} %tiles.9, bf16[3072,128]{1,0:T(8,128)(2,1)S(1)} %gather_rows.1.refs_0_, bf16[3072,128]{1,0:T(8,128)(2,1)S(1)} %collective-permute-done.2.refs_1_, ...), custom_call_target="tpu_custom_call" | custom-call | flops 629145600 | bytes 4915200 | tf_op jit(solution)/shard_map/forward_group/pallas_call | solution.py:142
  87.4 0.9 copy-done.1
  89.0 4.3 %collective-permute-done.7.refs_1_ = bf16[3072,128]{1,0:T(8,128)(2,1)S(1)} collective-permute-done((bf16[3072,128]{1,0:T(8,128)(2,1)S(1)}, bf16[3072,128]{1,0:T(8,128)(2,1)S(1)}, u32[]{:S(2)}, u32[]{:S(2)}) %collective-permute-start.7) | collective-permute-done | bytes 786464 | tf_op jit(solution)/shard_map/ppermute | solution.py:214
  93.3 4.6 %forward_group.3 = (bf16[12,128,128]{2,1,0:T(8,128)(2,1)}, bf16[12,128,128]{2,1,0:T(8,128)(2,1)S(1)}) custom-call(s32[398]{0:T(512)S(1)} %broadcast_add_fusion.plan, s32[14]{0:T(128)S(1)} %pad_add_fusion.spans, bf16[384,128,128]{2,1,0:T(8,128)(2,1)} %tiles.9, bf16[3072,128]{1,0:T(8,128)(2,1)S(1)} %collective-permute-done.6.refs_0_, ...), custom_call_target="tpu_custom_call" | custom-call | flops 251658240 | bytes 1966080 | tf_op jit(solution)/shard_map/forward_group/pallas_call | solution.py:142
  97.9 0.7 collective-permute-start.16
  98.6 2.9 %collective-permute-start.13 = (bf16[1536,128]{1,0:T(8,128)(2,1)}, bf16[1536,128]{1,0:T(8,128)(2,1)}, u32[]{:S(2)}, u32[]{:S(2)}) collective-permute-start(bf16[1536,128]{1,0:T(8,128)(2,1)} %bitcast.2.refs_0_), channel_id=1, source_target_pairs={{0,2},{1,3},{2,0},{3,1},{4,6},{5,7},{6,4},{7,5},{8,10},{9,11},{10,... | collective-permute-start | bytes 1179656 | tf_op jit(solution)/shard_map/ppermute | solution.py:219
  101.5 0.8 copy-done.11
  102.3 8.6 %collective-permute-done.16.refs_2_ = bf16[1536,128]{1,0:T(8,128)(2,1)} collective-permute-done((bf16[1536,128]{1,0:T(8,128)(2,1)S(1)}, bf16[1536,128]{1,0:T(8,128)(2,1)}, u32[]{:S(2)}, u32[]{:S(2)}) %collective-permute-start.16) | collective-permute-done | bytes 393248 | tf_op jit(solution)/shard_map/ppermute | solution.py:219
  111.4 3.7 %collective-permute-done.13.refs_2_ = bf16[1536,128]{1,0:T(8,128)(2,1)} collective-permute-done((bf16[1536,128]{1,0:T(8,128)(2,1)}, bf16[1536,128]{1,0:T(8,128)(2,1)}, u32[]{:S(2)}, u32[]{:S(2)}) %collective-permute-start.13) | collective-permute-done | bytes 393248 | tf_op jit(solution)/shard_map/ppermute | solution.py:219
  115.2 1.1 copy-done.2
  116.3 1.0 copy-done.12
  117.3 3.9 %mix.3 = (bf16[1536,128]{1,0:T(8,128)(2,1)S(1)}, bf16[12,128,128]{2,1,0:T(8,128)(2,1)S(1)}, f32[4,128,128]{2,1,0:T(8,128)S(1)}) custom-call(s32[1]{0:T(128)} %bitcast.1.shard, bf16[1536,128]{1,0:T(8,128)(2,1)S(1)} %bitcast.15, bf16[1536,128]{1,0:T(8,128)(2,1)} %collective-permute-done.15.refs_1_, bf16[1536,128]{1,0:T(8,128)(2,1)} %collective-permute-done.16.refs_2_, ...), custom_call_target="tpu_custom_call" | custom-call | flops 1207959552 | bytes 6291456 | tf_op jit(solution)/shard_map/mix/pallas_call | solution.py:290
  121.9 1.0 copy-done.6
  122.9 4.1 %mix.2 = (bf16[1536,128]{1,0:T(8,128)(2,1)S(1)}, bf16[12,128,128]{2,1,0:T(8,128)(2,1)S(1)}, f32[4,128,128]{2,1,0:T(8,128)S(1)}) custom-call(s32[1]{0:T(128)} %bitcast.1.shard, bf16[1536,128]{1,0:T(8,128)(2,1)} %bitcast.2.refs_0_, bf16[1536,128]{1,0:T(8,128)(2,1)} %collective-permute-done.12.refs_1_, bf16[1536,128]{1,0:T(8,128)(2,1)} %collective-permute-done.13.refs_2_, ...), custom_call_target="tpu_custom_call" | custom-call | flops 1207959552 | bytes 6291456 | tf_op jit(solution)/shard_map/mix/pallas_call | solution.py:290
  127.0 4.8 %backward_group.3 = (bf16[24,128,128]{2,1,0:T(8,128)(2,1)}, bf16[24,128,128]{2,1,0:T(8,128)(2,1)S(1)}) custom-call(s32[398]{0:T(512)S(1)} %broadcast_add_fusion.plan, s32[14]{0:T(128)S(1)} %pad_add_fusion.spans, bf16[384,128,128]{2,1,0:T(8,128)(2,1)} %tiles.9, bf16[12,128,128]{2,1,0:T(8,128)(2,1)S(1)} %get-tuple-element.61.refs_0_, ...), custom_call_target="tpu_custom_call" | custom-call | flops 251658240 | bytes 1966080 | tf_op jit(solution)/shard_map/backward_group/pallas_call | solution.py:190
  132.0 4.0 %collective-permute-start.19 = (bf16[24,128,128]{2,1,0:T(8,128)(2,1)S(1)}, bf16[24,128,128]{2,1,0:T(8,128)(2,1)S(1)}, u32[]{:S(2)}, u32[]{:S(2)}) collective-permute-start(bf16[24,128,128]{2,1,0:T(8,128)(2,1)S(1)} %get-tuple-element.65), channel_id=1, source_target_pairs={{4,8},{8,4},{12,16},{16,12},{20,24},{24,20},{28,32},{32,28},{36,40... | collective-permute-start | bytes 2359304 | tf_op jit(solution)/shard_map/ppermute | solution.py:214
  136.0 0.7 add.70
  136.7 5.1 %all-to-all-start = ((f32[64,8,128]{2,1,0:T(8,128)}), f32[64,8,128]{2,1,0:T(8,128)S(1)}, u32[]{:S(2)}, u32[]{:S(2)}) async-start(f32[64,8,128]{2,1,0:T(8,128)} %bitcast.4), calls=%async_computation | async-start | bytes 524288 | tf_op jit(solution)/shard_map/all_to_all | solution.py:356
  141.8 4.3 %backward_group.4 = (bf16[24,128,128]{2,1,0:T(8,128)(2,1)S(1)}, bf16[24,128,128]{2,1,0:T(8,128)(2,1)S(1)}) custom-call(s32[398]{0:T(512)S(1)} %broadcast_add_fusion.plan, s32[14]{0:T(128)S(1)} %pad_add_fusion.spans, bf16[384,128,128]{2,1,0:T(8,128)(2,1)} %tiles.9, bf16[12,128,128]{2,1,0:T(8,128)(2,1)S(1)} %get-tuple-element.61.refs_0_, ...), custom_call_target="tpu_custom_call" | custom-call | flops 251658240 | bytes 1966080 | tf_op jit(solution)/shard_map/backward_group/pallas_call | solution.py:190
  146.1 7.8 %collective-permute-done.18.carried = bf16[24,128,128]{2,1,0:T(8,128)(2,1)S(1)} collective-permute-done((bf16[24,128,128]{2,1,0:T(8,128)(2,1)}, bf16[24,128,128]{2,1,0:T(8,128)(2,1)S(1)}, u32[]{:S(2)}, u32[]{:S(2)}) %collective-permute-start.18) | collective-permute-done | bytes 786464 | tf_op jit(solution)/shard_map/ppermute | solution.py:214
  153.9 7.1 %collective-permute-done.19.carried = bf16[24,128,128]{2,1,0:T(8,128)(2,1)S(1)} collective-permute-done((bf16[24,128,128]{2,1,0:T(8,128)(2,1)S(1)}, bf16[24,128,128]{2,1,0:T(8,128)(2,1)S(1)}, u32[]{:S(2)}, u32[]{:S(2)}) %collective-permute-start.19) | collective-permute-done | bytes 786464 | tf_op jit(solution)/shard_map/ppermute | solution.py:214
  161.1 1.1 add_part.6
  162.3 4.0 %collective-permute-start.20 = (bf16[24,128,128]{2,1,0:T(8,128)(2,1)S(1)}, bf16[24,128,128]{2,1,0:T(8,128)(2,1)}, u32[]{:S(2)}, u32[]{:S(2)}) collective-permute-start(bf16[24,128,128]{2,1,0:T(8,128)(2,1)S(1)} %add_part.4), channel_id=1, source_target_pairs={{4,8},{8,4},{12,16},{16,12},{20,24},{24,20},{28,32},{32,28},{36,40... | collective-permute-start | bytes 2359304 | tf_op jit(solution)/shard_map/ppermute | solution.py:214
  166.4 0.7 broadcast_in_dim.69
  167.2 5.2 %all-to-all-start.1 = ((f32[64,8,128]{2,1,0:T(8,128)}), f32[64,8,128]{2,1,0:T(8,128)S(1)}, u32[]{:S(2)}, u32[]{:S(2)}) async-start(f32[64,8,128]{2,1,0:T(8,128)} %broadcast_in_dim.69), calls=%async_computation.1 | async-start | bytes 524288 | tf_op jit(solution)/shard_map/all_to_all | solution.py:361
  172.4 5.8 %backward_group.5 = (f32[24,128,128]{2,1,0:T(8,128)S(1)}, bf16[24,128,128]{2,1,0:T(8,128)(2,1)S(1)}, bf16[24,128,128]{2,1,0:T(8,128)(2,1)S(1)}) custom-call(s32[398]{0:T(512)S(1)} %broadcast_add_fusion.plan, s32[14]{0:T(128)S(1)} %pad_add_fusion.spans, bf16[384,128,128]{2,1,0:T(8,128)(2,1)} %tiles.9, bf16[12,128,128]{2,1,0:T(8,128)(2,1)S(1)} %get-tuple-element.61.refs_0_, ...), custom_call_target="tpu_custom_call" | custom-call | flops 377487360 | bytes 2949120 | tf_op jit(solution)/shard_map/backward_group/pallas_call | solution.py:190
  178.2 5.6 %collective-permute-done.22.carried = bf16[24,128,128]{2,1,0:T(8,128)(2,1)} collective-permute-done((bf16[24,128,128]{2,1,0:T(8,128)(2,1)}, bf16[24,128,128]{2,1,0:T(8,128)(2,1)}, u32[]{:S(2)}, u32[]{:S(2)}) %collective-permute-start.22) | collective-permute-done | bytes 786464 | tf_op jit(solution)/shard_map/ppermute | solution.py:214
  183.7 2.2 %add_part.7 = bf16[24,128,128]{2,1,0:T(8,128)(2,1)} custom-call(bf16[24,128,128]{2,1,0:T(8,128)(2,1)} %collective-permute-done.22.carried, bf16[24,128,128]{2,1,0:T(8,128)(2,1)S(1)} %get-tuple-element.72.own), custom_call_target="tpu_custom_call" | custom-call | bytes 2359296 | tf_op jit(solution)/shard_map/add_part/pallas_call | solution.py:313
  185.9 4.3 %collective-permute-start.23 = (bf16[24,128,128]{2,1,0:T(8,128)(2,1)}, bf16[24,128,128]{2,1,0:T(8,128)(2,1)S(1)}, u32[]{:S(2)}, u32[]{:S(2)}) collective-permute-start(bf16[24,128,128]{2,1,0:T(8,128)(2,1)} %add_part.7), channel_id=1, source_target_pairs={{4,8},{8,4},{12,16},{16,12},{20,24},{24,20},{28,32},{32,28},{36,40... | collective-permute-start | bytes 2359304 | tf_op jit(solution)/shard_map/ppermute | solution.py:214
  190.7 2.2 %add_part.5 = bf16[24,128,128]{2,1,0:T(8,128)(2,1)} custom-call(bf16[24,128,128]{2,1,0:T(8,128)(2,1)} %collective-permute-done.20.carried, bf16[24,128,128]{2,1,0:T(8,128)(2,1)S(1)} %get-tuple-element.69.own), custom_call_target="tpu_custom_call" | custom-call | bytes 2359296 | tf_op jit(solution)/shard_map/add_part/pallas_call | solution.py:313
  192.9 0.9 pad_maximum_fusion
  193.9 0.7 pad_maximum_fusion.1
  194.6 13.6 %collective-permute-done.23.right = bf16[24,128,128]{2,1,0:T(8,128)(2,1)S(1)} collective-permute-done((bf16[24,128,128]{2,1,0:T(8,128)(2,1)}, bf16[24,128,128]{2,1,0:T(8,128)(2,1)S(1)}, u32[]{:S(2)}, u32[]{:S(2)}) %collective-permute-start.23) | collective-permute-done | bytes 786464 | tf_op jit(solution)/shard_map/ppermute | solution.py:214
  208.3 6.8 %scatter_rows.1 = bf16[3072,128]{1,0:T(8,128)(2,1)} custom-call(s32[3072]{0:T(1024)S(1)} %copy-done.14, s32[1]{0:T(128)} %bitcast.base, f32[24,128,128]{2,1,0:T(8,128)S(1)} %get-tuple-element.76.own, bf16[24,128,128]{2,1,0:T(8,128)(2,1)S(1)} %collective-permute-done.21.left, bf16[24,128,128]{2,1,0:T(8,128)(2,1)S(1)} %collective-permute-done.23.right), custom_call_target="tpu_custom_call" | custom-call | bytes 12582912 | tf_op jit(solution)/shard_map/scatter_rows/pallas_call | solution.py:342
  (69 shorter events, 5.2 us)
Async XLA Ops:
  0.6 56.0 %copy-start = (bf16[3072,128]{1,0:T(8,128)(2,1)S(1)}, bf16[3072,128]{1,0:T(8,128)(2,1)}, u32[]{:S(2)}) copy-start(bf16[3072,128]{1,0:T(8,128)(2,1)} %refs_4_.1) | copy-start | bytes 2359300
  0.6 23.9 %collective-permute-start = (bf16[3072,128]{1,0:T(8,128)(2,1)}, bf16[3072,128]{1,0:T(8,128)(2,1)S(1)}, u32[]{:S(2)}, u32[]{:S(2)}) collective-permute-start(bf16[3072,128]{1,0:T(8,128)(2,1)} %refs_4_.1), channel_id=1, source_target_pairs={{0,2},{1,3},{2,0},{3,1},{4,6},{5,7},{6,4},{7,5},{8,10},{9,11},{10,... | collective-permute-start | bytes 2359304 | tf_op jit(solution)/shard_map/ppermute | solution.py:219
  2.8 21.7 %collective-permute-start.1 = (bf16[128,512]{1,0:T(8,128)(2,1)}, bf16[128,512]{1,0:T(8,128)(2,1)S(1)}, u32[]{:S(2)}, u32[]{:S(2)}) collective-permute-start(bf16[128,512]{1,0:T(8,128)(2,1)} %refs_8_.1), channel_id=1, source_target_pairs={{0,2},{1,3},{2,0},{3,1},{4,6},{5,7},{6,4},{7,5},{8,10},{9,11},{10,... | collective-permute-start | bytes 393224 | tf_op jit(solution)/shard_map/ppermute | solution.py:219
  4.3 1.1 copy-start.3
  5.4 0.7 copy-start.13
  6.1 5.1 %copy-start.15 = (s32[384]{0:T(512)S(1)}, s32[384]{0:T(512)}, u32[]{:S(2)}) copy-start(s32[384]{0:T(512)} %param.9) | copy-start | bytes 4612
  6.1 5.1 %copy-start.16 = (s32[384]{0:T(512)S(1)}, s32[384]{0:T(512)}, u32[]{:S(2)}) copy-start(s32[384]{0:T(512)} %param.10) | copy-start | bytes 4612
  6.1 72.0 %copy-start.4 = (bf16[128,512]{1,0:T(8,128)(2,1)S(1)}, bf16[128,512]{1,0:T(8,128)(2,1)}, u32[]{:S(2)}) copy-start(bf16[128,512]{1,0:T(8,128)(2,1)} %refs_8_.1) | copy-start | bytes 393220
  24.5 18.6 %collective-permute-start.2 = (bf16[3072,128]{1,0:T(8,128)(2,1)S(1)}, bf16[3072,128]{1,0:T(8,128)(2,1)S(1)}, u32[]{:S(2)}, u32[]{:S(2)}) collective-permute-start(bf16[3072,128]{1,0:T(8,128)(2,1)S(1)} %gather_rows.1.refs_0_), channel_id=1, source_target_pairs={{0,4},{4,0},{8,12},{12,8},{16,20},{20,16},{24,28},{28,24},{32,36},... | collective-permute-start | bytes 2359304 | tf_op jit(solution)/shard_map/ppermute | solution.py:214
  26.5 24.2 %collective-permute-start.3 = (bf16[3072,128]{1,0:T(8,128)(2,1)S(1)}, bf16[3072,128]{1,0:T(8,128)(2,1)S(1)}, u32[]{:S(2)}, u32[]{:S(2)}) collective-permute-start(bf16[3072,128]{1,0:T(8,128)(2,1)S(1)} %gather_rows.1.refs_0_), channel_id=1, source_target_pairs={{4,8},{8,4},{12,16},{16,12},{20,24},{24,20},{28,32},{32,28},{36,40... | collective-permute-start | bytes 2359304 | tf_op jit(solution)/shard_map/ppermute | solution.py:214
  50.7 17.5 %collective-permute-start.4 = (bf16[3072,128]{1,0:T(8,128)(2,1)S(1)}, bf16[3072,128]{1,0:T(8,128)(2,1)S(1)}, u32[]{:S(2)}, u32[]{:S(2)}) collective-permute-start(bf16[3072,128]{1,0:T(8,128)(2,1)S(1)} %collective-permute-done.3.refs_2_), channel_id=1, source_target_pairs={{0,4},{4,0},{8,12},{12,8},{16,20},{20,16},{24,28},{28,24},{32,36},... | collective-permute-start | bytes 2359304 | tf_op jit(solution)/shard_map/ppermute | solution.py:214
  50.7 21.7 %collective-permute-start.5 = (bf16[3072,128]{1,0:T(8,128)(2,1)S(1)}, bf16[3072,128]{1,0:T(8,128)(2,1)S(1)}, u32[]{:S(2)}, u32[]{:S(2)}) collective-permute-start(bf16[3072,128]{1,0:T(8,128)(2,1)S(1)} %collective-permute-done.2.refs_1_), channel_id=1, source_target_pairs={{4,8},{8,4},{12,16},{16,12},{20,24},{24,20},{28,32},{32,28},{36,40... | collective-permute-start | bytes 2359304 | tf_op jit(solution)/shard_map/ppermute | solution.py:214
  56.7 30.7 %collective-permute-start.10 = (bf16[3072,128]{1,0:T(8,128)(2,1)S(1)}, bf16[3072,128]{1,0:T(8,128)(2,1)S(1)}, u32[]{:S(2)}, u32[]{:S(2)}) collective-permute-start(bf16[3072,128]{1,0:T(8,128)(2,1)S(1)} %copy-done), channel_id=1, source_target_pairs={{0,1},{1,0},{2,3},{3,2},{4,5},{5,4},{6,7},{7,6},{8,9},{9,8},{10,11... | collective-permute-start | bytes 2359304 | tf_op jit(solution)/shard_map/ppermute | solution.py:219
  56.7 30.7 %collective-permute-start.11 = (bf16[3072,128]{1,0:T(8,128)(2,1)S(1)}, bf16[3072,128]{1,0:T(8,128)(2,1)S(1)}, u32[]{:S(2)}, u32[]{:S(2)}) collective-permute-start(bf16[3072,128]{1,0:T(8,128)(2,1)S(1)} %collective-permute-done.refs_6_), channel_id=1, source_target_pairs={{0,1},{1,0},{2,3},{3,2},{4,5},{5,4},{6,7},{7,6},{8,9},{9,8},{10,11... | collective-permute-start | bytes 2359304 | tf_op jit(solution)/shard_map/ppermute | solution.py:219
  72.4 16.6 %collective-permute-start.6 = (bf16[3072,128]{1,0:T(8,128)(2,1)S(1)}, bf16[3072,128]{1,0:T(8,128)(2,1)S(1)}, u32[]{:S(2)}, u32[]{:S(2)}) collective-permute-start(bf16[3072,128]{1,0:T(8,128)(2,1)S(1)} %collective-permute-done.5.refs_4_), channel_id=1, source_target_pairs={{0,4},{4,0},{8,12},{12,8},{16,20},{20,16},{24,28},{28,24},{32,36},... | collective-permute-start | bytes 2359304 | tf_op jit(solution)/shard_map/ppermute | solution.py:214
  72.4 20.9 %collective-permute-start.7 = (bf16[3072,128]{1,0:T(8,128)(2,1)S(1)}, bf16[3072,128]{1,0:T(8,128)(2,1)S(1)}, u32[]{:S(2)}, u32[]{:S(2)}) collective-permute-start(bf16[3072,128]{1,0:T(8,128)(2,1)S(1)} %collective-permute-done.4.refs_3_), channel_id=1, source_target_pairs={{4,8},{8,4},{12,16},{16,12},{20,24},{24,20},{28,32},{32,28},{36,40... | collective-permute-start | bytes 2359304 | tf_op jit(solution)/shard_map/ppermute | solution.py:214
  78.1 1.3 collective-permute-start.8
  79.5 7.9 %collective-permute-start.9 = (bf16[128,512]{1,0:T(8,128)(2,1)S(1)}, bf16[128,512]{1,0:T(8,128)(2,1)S(1)}, u32[]{:S(2)}, u32[]{:S(2)}) collective-permute-start(bf16[128,512]{1,0:T(8,128)(2,1)S(1)} %collective-permute-done.1.refs_10_), channel_id=1, source_target_pairs={{0,1},{1,0},{2,3},{3,2},{4,5},{5,4},{6,7},{7,6},{8,9},{9,8},{10,11... | collective-permute-start | bytes 393224 | tf_op jit(solution)/shard_map/ppermute | solution.py:219
  87.4 0.9 copy-start.1
  97.9 13.0 %collective-permute-start.16 = (bf16[1536,128]{1,0:T(8,128)(2,1)S(1)}, bf16[1536,128]{1,0:T(8,128)(2,1)}, u32[]{:S(2)}, u32[]{:S(2)}) collective-permute-start(bf16[1536,128]{1,0:T(8,128)(2,1)S(1)} %bitcast.13), channel_id=1, source_target_pairs={{0,2},{1,3},{2,0},{3,1},{4,6},{5,7},{6,4},{7,5},{8,10},{9,11},{10,... | collective-permute-start | bytes 1179656 | tf_op jit(solution)/shard_map/ppermute | solution.py:219
  98.6 16.5 %collective-permute-start.13 = (bf16[1536,128]{1,0:T(8,128)(2,1)}, bf16[1536,128]{1,0:T(8,128)(2,1)}, u32[]{:S(2)}, u32[]{:S(2)}) collective-permute-start(bf16[1536,128]{1,0:T(8,128)(2,1)} %bitcast.2.refs_0_), channel_id=1, source_target_pairs={{0,2},{1,3},{2,0},{3,1},{4,6},{5,7},{6,4},{7,5},{8,10},{9,11},{10,... | collective-permute-start | bytes 1179656 | tf_op jit(solution)/shard_map/ppermute | solution.py:219
  101.5 13.6 %collective-permute-start.15 = (bf16[1536,128]{1,0:T(8,128)(2,1)S(1)}, bf16[1536,128]{1,0:T(8,128)(2,1)}, u32[]{:S(2)}, u32[]{:S(2)}) collective-permute-start(bf16[1536,128]{1,0:T(8,128)(2,1)S(1)} %bitcast.14), channel_id=1, source_target_pairs={{0,1},{1,0},{2,3},{3,2},{4,5},{5,4},{6,7},{7,6},{8,9},{9,8},{10,11... | collective-permute-start | bytes 1179656 | tf_op jit(solution)/shard_map/ppermute | solution.py:219
  101.5 0.8 copy-start.11
  110.9 4.2 %collective-permute-start.17 = (bf16[1536,128]{1,0:T(8,128)(2,1)}, bf16[1536,128]{1,0:T(8,128)(2,1)}, u32[]{:S(2)}, u32[]{:S(2)}) collective-permute-start(bf16[1536,128]{1,0:T(8,128)(2,1)} %collective-permute-done.16.refs_2_), channel_id=1, source_target_pairs={{0,1},{1,0},{2,3},{3,2},{4,5},{5,4},{6,7},{7,6},{8,9},{9,8},{10,11... | collective-permute-start | bytes 1179656 | tf_op jit(solution)/shard_map/ppermute | solution.py:219
  110.9 11.0 %collective-permute-start.12 = (bf16[1536,128]{1,0:T(8,128)(2,1)}, bf16[1536,128]{1,0:T(8,128)(2,1)}, u32[]{:S(2)}, u32[]{:S(2)}) collective-permute-start(bf16[1536,128]{1,0:T(8,128)(2,1)} %bitcast.2.refs_0_), channel_id=1, source_target_pairs={{0,1},{1,0},{2,3},{3,2},{4,5},{5,4},{6,7},{7,6},{8,9},{9,8},{10,11... | collective-permute-start | bytes 1179656 | tf_op jit(solution)/shard_map/ppermute | solution.py:219
  115.1 6.8 %collective-permute-start.14 = (bf16[1536,128]{1,0:T(8,128)(2,1)}, bf16[1536,128]{1,0:T(8,128)(2,1)}, u32[]{:S(2)}, u32[]{:S(2)}) collective-permute-start(bf16[1536,128]{1,0:T(8,128)(2,1)} %collective-permute-done.13.refs_2_), channel_id=1, source_target_pairs={{0,1},{1,0},{2,3},{3,2},{4,5},{5,4},{6,7},{7,6},{8,9},{9,8},{10,11... | collective-permute-start | bytes 1179656 | tf_op jit(solution)/shard_map/ppermute | solution.py:219
  115.1 1.1 copy-start.2
  116.3 1.0 copy-start.12
  121.2 0.7 copy-start.5
  121.9 5.1 %copy-start.7 = (bf16[1536,128]{1,0:T(8,128)(2,1)}, bf16[1536,128]{1,0:T(8,128)(2,1)S(1)}, u32[]{:S(2)}) copy-start(bf16[1536,128]{1,0:T(8,128)(2,1)S(1)} %get-tuple-element.74) | copy-start | bytes 1179652
  121.9 1.0 copy-start.6
  127.0 4.9 %copy-start.9 = (bf16[1536,128]{1,0:T(8,128)(2,1)}, bf16[1536,128]{1,0:T(8,128)(2,1)S(1)}, u32[]{:S(2)}) copy-start(bf16[1536,128]{1,0:T(8,128)(2,1)S(1)} %get-tuple-element.73) | copy-start | bytes 1179652
  131.9 22.0 %collective-permute-start.18 = (bf16[24,128,128]{2,1,0:T(8,128)(2,1)}, bf16[24,128,128]{2,1,0:T(8,128)(2,1)S(1)}, u32[]{:S(2)}, u32[]{:S(2)}) collective-permute-start(bf16[24,128,128]{2,1,0:T(8,128)(2,1)} %get-tuple-element.64), channel_id=1, source_target_pairs={{0,4},{4,0},{8,12},{12,8},{16,20},{20,16},{24,28},{28,24},{32,36},... | collective-permute-start | bytes 2359304 | tf_op jit(solution)/shard_map/ppermute | solution.py:214
  132.0 29.1 %collective-permute-start.19 = (bf16[24,128,128]{2,1,0:T(8,128)(2,1)S(1)}, bf16[24,128,128]{2,1,0:T(8,128)(2,1)S(1)}, u32[]{:S(2)}, u32[]{:S(2)}) collective-permute-start(bf16[24,128,128]{2,1,0:T(8,128)(2,1)S(1)} %get-tuple-element.65), channel_id=1, source_target_pairs={{4,8},{8,4},{12,16},{16,12},{20,24},{24,20},{28,32},{32,28},{36,40... | collective-permute-start | bytes 2359304 | tf_op jit(solution)/shard_map/ppermute | solution.py:214
  136.7 29.6 %all-to-all-start = ((f32[64,8,128]{2,1,0:T(8,128)}), f32[64,8,128]{2,1,0:T(8,128)S(1)}, u32[]{:S(2)}, u32[]{:S(2)}) async-start(f32[64,8,128]{2,1,0:T(8,128)} %bitcast.4), calls=%async_computation | async-start | bytes 524288 | tf_op jit(solution)/shard_map/all_to_all | solution.py:356
  162.1 21.6 %collective-permute-start.22 = (bf16[24,128,128]{2,1,0:T(8,128)(2,1)}, bf16[24,128,128]{2,1,0:T(8,128)(2,1)}, u32[]{:S(2)}, u32[]{:S(2)}) collective-permute-start(bf16[24,128,128]{2,1,0:T(8,128)(2,1)} %add_part.6), channel_id=1, source_target_pairs={{0,4},{4,0},{8,12},{12,8},{16,20},{20,16},{24,28},{28,24},{32,36},... | collective-permute-start | bytes 2359304 | tf_op jit(solution)/shard_map/ppermute | solution.py:214
  162.3 28.4 %collective-permute-start.20 = (bf16[24,128,128]{2,1,0:T(8,128)(2,1)S(1)}, bf16[24,128,128]{2,1,0:T(8,128)(2,1)}, u32[]{:S(2)}, u32[]{:S(2)}) collective-permute-start(bf16[24,128,128]{2,1,0:T(8,128)(2,1)S(1)} %add_part.4), channel_id=1, source_target_pairs={{4,8},{8,4},{12,16},{16,12},{20,24},{24,20},{28,32},{32,28},{36,40... | collective-permute-start | bytes 2359304 | tf_op jit(solution)/shard_map/ppermute | solution.py:214
  167.2 26.7 %all-to-all-start.1 = ((f32[64,8,128]{2,1,0:T(8,128)}), f32[64,8,128]{2,1,0:T(8,128)S(1)}, u32[]{:S(2)}, u32[]{:S(2)}) async-start(f32[64,8,128]{2,1,0:T(8,128)} %broadcast_in_dim.69), calls=%async_computation.1 | async-start | bytes 524288 | tf_op jit(solution)/shard_map/all_to_all | solution.py:361
  185.9 7.0 %copy-start.8 = (bf16[1536,128]{1,0:T(8,128)(2,1)S(1)}, bf16[1536,128]{1,0:T(8,128)(2,1)}, u32[]{:S(2)}) copy-start(bf16[1536,128]{1,0:T(8,128)(2,1)} %copy-done.7) | copy-start | bytes 1179652
  185.9 7.0 %copy-start.10 = (bf16[1536,128]{1,0:T(8,128)(2,1)S(1)}, bf16[1536,128]{1,0:T(8,128)(2,1)}, u32[]{:S(2)}) copy-start(bf16[1536,128]{1,0:T(8,128)(2,1)} %copy-done.9) | copy-start | bytes 1179652
  185.9 22.3 %collective-permute-start.23 = (bf16[24,128,128]{2,1,0:T(8,128)(2,1)}, bf16[24,128,128]{2,1,0:T(8,128)(2,1)S(1)}, u32[]{:S(2)}, u32[]{:S(2)}) collective-permute-start(bf16[24,128,128]{2,1,0:T(8,128)(2,1)} %add_part.7), channel_id=1, source_target_pairs={{4,8},{8,4},{12,16},{16,12},{20,24},{24,20},{28,32},{32,28},{36,40... | collective-permute-start | bytes 2359304 | tf_op jit(solution)/shard_map/ppermute | solution.py:214
  192.9 15.4 %copy-start.14 = (s32[3072]{0:T(1024)S(1)}, s32[3072]{0:T(1024)}, u32[]{:S(2)}) copy-start(s32[3072]{0:T(1024)} %perm.3) | copy-start | bytes 36868
  192.9 15.4 %collective-permute-start.21 = (bf16[24,128,128]{2,1,0:T(8,128)(2,1)}, bf16[24,128,128]{2,1,0:T(8,128)(2,1)S(1)}, u32[]{:S(2)}, u32[]{:S(2)}) collective-permute-start(bf16[24,128,128]{2,1,0:T(8,128)(2,1)} %add_part.5), channel_id=1, source_target_pairs={{0,4},{4,0},{8,12},{12,8},{16,20},{20,16},{24,28},{28,24},{32,36},... | collective-permute-start | bytes 2359304 | tf_op jit(solution)/shard_map/ppermute | solution.py:214

commit v3 on v2

--- a/solution.py
+++ b/solution.py
@@ -10,6 +10,7 @@
 ROW_PARTS = 2
 GROUPS = (2 * REACH + 1) * PARTS
 wide_step = 8
+together = 4
 narrow_step = 2
 ring = 32
 row_bits = 5
@@ -224,32 +225,31 @@
     return [value, exchange(value, 1), far, exchange(far, 1)]
 
 
-def gather_kernel(part, perm, base, source, out, wide, moved):
+def gather_kernel(part, perm, source, out, wide, moved):
     rows = out.shape[0]
     wide[...] = source[...].astype(f32)
-    first = base[0]
 
     @pl.loop(0, rows // 16)
     def _(step):
         at = step * 16
         for j in range(16):
-            moved[pl.ds(at + j, 1), :] = wide[pl.ds(perm[part * rows + at + j] - first, 1), :]
+            moved[pl.ds(at + j, 1), :] = wide[pl.ds(perm[part * rows + at + j], 1), :]
 
     out[...] = moved[...].astype(out.dtype)
 
 
-def gather_rows(part, perm, base, source):
+def gather_rows(part, perm, source):
     shape = (perm.shape[0] // PARTS, source.shape[1])
     return pl.pallas_call(
         functools.partial(gather_kernel, part),
         out_shape=pltpu.VMEM(shape, source.dtype),
-        in_specs=[SMEM, SMEM, VMEM],
+        in_specs=[SMEM, VMEM],
         out_specs=VMEM,
         scratch_shapes=[pltpu.VMEM(source.shape, f32), pltpu.VMEM(shape, f32)],
         cost_estimate=pl.CostEstimate(flops=0, bytes_accessed=12 * 2**20, transcendentals=0),
         compiler_params=pltpu.CompilerParams(vmem_limit_bytes=8 * 2**20),
         name="gather_rows",
-    )(perm, base, source)
+    )(perm, source)
 
 
 def mix_kernel(part, block_rows, shard, *refs):
@@ -321,34 +321,35 @@
     )(*near(carried, own))
 
 
-def scatter_kernel(perm, base, own, left, right, out, moved, wide):
-    first = base[0]
+def scatter_kernel(perm, own, left, right, out, moved, wide):
     blocks, width, side = own.shape
 
-    @pl.loop(0, blocks)
-    def _(b):
-        total = own[b] + left[b].astype(f32) + right[b].astype(f32)
-        wide[...] = total.T
-        at = b * side
-        for j in range(side):
-            moved[pl.ds(perm[at + j] - first, 1), :] = wide[j : j + 1, :]
+    @pl.loop(0, blocks // together)
+    def _(step):
+        for k in range(together):
+            b = step * together + k
+            wide[k] = (own[b] + left[b].astype(f32) + right[b].astype(f32)).T
+        for k in range(together):
+            at = (step * together + k) * side
+            for j in range(side):
+                moved[pl.ds(perm[at + j], 1), :] = wide[k, j : j + 1, :]
 
     out[...] = moved[...].astype(out.dtype)
 
 
-def scatter_rows(perm, base, own, left, right):
+def scatter_rows(perm, own, left, right):
     width = own.shape[1]
     rows = perm.shape[0]
     return pl.pallas_call(
         scatter_kernel,
         out_shape=jax.ShapeDtypeStruct((rows, width), bf16),
-        in_specs=[SMEM, SMEM] + [VMEM] * 3,
+        in_specs=[SMEM] + [VMEM] * 3,
         out_specs=VMEM,
-        scratch_shapes=[pltpu.VMEM((rows, width), f32), pltpu.VMEM((own.shape[2], width), f32)],
+        scratch_shapes=[pltpu.VMEM((rows, width), f32), pltpu.VMEM((together, own.shape[2], width), f32)],
         cost_estimate=pl.CostEstimate(flops=0, bytes_accessed=12 * 2**20, transcendentals=0),
         compiler_params=pltpu.CompilerParams(vmem_limit_bytes=8 * 2**20),
         name="scatter_rows",
-    )(perm, base, *near(own, left, right))
+    )(perm, *near(own, left, right))
 
 
 def sum_share(value):
@@ -367,7 +368,7 @@
     blocks = rows // side
     devices = lax.axis_size("vertex")
     here = lax.axis_index("vertex")
-    base = (here * rows).astype(jnp.int32).reshape(1)
+    local = permutation - here * rows
     shard = lax.axis_index("feat").astype(jnp.int32).reshape(1)
     span = rows // ROW_PARTS
     scale = 1.0 / math.sqrt(rows * devices)
@@ -375,7 +376,7 @@
 
     far = exchange(cotangent, 2)
     weight_far = exchange(weight, 2)
-    ordered = gather_rows(0, permutation, base, features)
+    ordered = gather_rows(0, local, features)
     plan, spans = slot_plan(tile_row, tile_col, here, blocks, devices)
     ordered, far, weight_far = lax.optimization_barrier((ordered, far, weight_far))
 
@@ -415,7 +416,7 @@
     share = spread_shares(after(even, share), scale)
     even, odd = swap(even, 0), swap(odd, 1)
     even, odd, activations = lax.optimization_barrier((even, odd, activations))
-    grad_features = scatter_rows(permutation, base, own[0], even, odd)
+    grad_features = scatter_rows(local, own[0], even, odd)
     share = share.reshape(-1, width, width)
     grad_weight = jnp.concatenate([share[k] for k in range(share.shape[0])], axis=1)
     return (activations, grad_features, grad_weight)

time: 216 us -> 216 us (level)
  Pallas kernels: 52.7 us -> 45.8 us
  starting transfers between devices: 52.5 us -> 59.3 us
    ppermute x12, starting transfers between devices: 33.8 us -> 40.5 us  [swap(): return lax.ppermute(value, 'vertex', pairs)]
    pallas_call x2, Pallas kernels: 12.3 us -> 10.1 us  [forward_group(): pl.pallas_call(functools.partial(forward_kernel, groups, first, last), ou...]
    unnamed x34 -> x36, local copies, waits for them, and re-layouts: 7.32 us -> 6.63 us
  transfers between devices with their start and end apart: 26 -> 26, of which waited for: 16 -> 15; matrix products, arithmetic and copies ran while one was open for 2% -> 2% of each run, Pallas kernels for 15% -> 13%
where the time goes in v3:
time: 216 us; the launch traced here: 214 us
  waiting for transfers between devices  96.7 us (45%)
  starting transfers between devices  59.3 us (27%)
  Pallas kernels  45.8 us (21%)
  local copies, waits for them, and re-layouts  7.38 us (3%)
  other arithmetic  4.02 us (2%)
    ppermute x12, waiting for transfers between devices, swap(): return lax.ppermute(value, 'vertex', pairs)  69 us
    ppermute x12, starting transfers between devices, swap(): return lax.ppermute(value, 'vertex', pairs)  40.5 us
    ppermute x12, waiting for transfers between devices, exchange(): lax.ppermute(value, 'feat', [(source, source ^ step) for source in range(...  27.7 us
    pallas_call x3, Pallas kernels, backward_group(): pl.pallas_call(functools.partial(backward_kernel, groups), out_shape=[plt...  12.9 us
    pallas_call x2, Pallas kernels, forward_group(): pl.pallas_call(functools.partial(forward_kernel, groups, first, last), ou...  10.1 us
    ppermute x12, starting transfers between devices, exchange(): lax.ppermute(value, 'feat', [(source, source ^ step) for source in range(...  8.41 us
    pallas_call x2, Pallas kernels, mix(): pl.pallas_call(functools.partial(mix_kernel, part, block_rows), out_shape...  8 us
    unnamed x36, local copies, waits for them, and re-layouts  6.63 us
  transfers between devices with their start and end apart: 26, of which 15 were waited for; matrix products, arithmetic and copies ran while one was open for 2% of the time, Pallas kernels for 13%

profile of v3, /device:TPU:16, one launch (start us, length us, event | category | flops | bytes accessed | tf_op | source)
XLA Modules:
  0.0 214.1 jit_solution(17617002045121767595)
XLA Ops:
  0.6 2.2 %collective-permute-start = (bf16[3072,128]{1,0:T(8,128)(2,1)}, bf16[3072,128]{1,0:T(8,128)(2,1)S(1)}, u32[]{:S(2)}, u32[]{:S(2)}) collective-permute-start(bf16[3072,128]{1,0:T(8,128)(2,1)} %refs_4_.1), channel_id=1, source_target_pairs={{0,2},{1,3},{2,0},{3,1},{4,6},{5,7},{6,4},{7,5},{8,10},{9,11},{10,... | collective-permute-start | bytes 2359304 | tf_op jit(solution)/shard_map/ppermute | solution.py:220
  2.8 1.5 collective-permute-start.1
  5.0 1.1 copy-done.3
  6.1 4.1 %gather_rows.1.refs_0_ = bf16[3072,128]{1,0:T(8,128)(2,1)S(1)} custom-call(s32[3072]{0:T(1024)S(1)} %broadcast_subtract_fusion.perm, bf16[3072,128]{1,0:T(8,128)(2,1)S(1)} %copy-done.3), custom_call_target="tpu_custom_call" | custom-call | bytes 12582912 | tf_op jit(solution)/shard_map/gather_rows/pallas_call | solution.py:243
  10.6 13.9 %collective-permute-done.1.refs_10_ = bf16[128,512]{1,0:T(8,128)(2,1)S(1)} collective-permute-done((bf16[128,512]{1,0:T(8,128)(2,1)}, bf16[128,512]{1,0:T(8,128)(2,1)S(1)}, u32[]{:S(2)}, u32[]{:S(2)}) %collective-permute-start.1) | collective-permute-done | bytes 131104 | tf_op jit(solution)/shard_map/ppermute | solution.py:220
  24.5 1.9 collective-permute-start.2
  26.5 7.9 %collective-permute-start.3 = (bf16[3072,128]{1,0:T(8,128)(2,1)S(1)}, bf16[3072,128]{1,0:T(8,128)(2,1)S(1)}, u32[]{:S(2)}, u32[]{:S(2)}) collective-permute-start(bf16[3072,128]{1,0:T(8,128)(2,1)S(1)} %gather_rows.1.refs_0_), channel_id=1, source_target_pairs={{4,8},{8,4},{12,16},{16,12},{20,24},{24,20},{28,32},{32,28},{36,40... | collective-permute-start | bytes 2359304 | tf_op jit(solution)/shard_map/ppermute | solution.py:215
  34.8 8.3 %collective-permute-done.2.refs_1_ = bf16[3072,128]{1,0:T(8,128)(2,1)S(1)} collective-permute-done((bf16[3072,128]{1,0:T(8,128)(2,1)S(1)}, bf16[3072,128]{1,0:T(8,128)(2,1)S(1)}, u32[]{:S(2)}, u32[]{:S(2)}) %collective-permute-start.2) | collective-permute-done | bytes 786464 | tf_op jit(solution)/shard_map/ppermute | solution.py:215
  43.1 7.6 %collective-permute-done.3.refs_2_ = bf16[3072,128]{1,0:T(8,128)(2,1)S(1)} collective-permute-done((bf16[3072,128]{1,0:T(8,128)(2,1)S(1)}, bf16[3072,128]{1,0:T(8,128)(2,1)S(1)}, u32[]{:S(2)}, u32[]{:S(2)}) %collective-permute-start.3) | collective-permute-done | bytes 786464 | tf_op jit(solution)/shard_map/ppermute | solution.py:215
  50.7 6.0 %collective-permute-start.5 = (bf16[3072,128]{1,0:T(8,128)(2,1)S(1)}, bf16[3072,128]{1,0:T(8,128)(2,1)S(1)}, u32[]{:S(2)}, u32[]{:S(2)}) collective-permute-start(bf16[3072,128]{1,0:T(8,128)(2,1)S(1)} %collective-permute-done.2.refs_1_), channel_id=1, source_target_pairs={{4,8},{8,4},{12,16},{16,12},{20,24},{24,20},{28,32},{32,28},{36,40... | collective-permute-start | bytes 2359304 | tf_op jit(solution)/shard_map/ppermute | solution.py:215
  57.2 11.0 %collective-permute-done.4.refs_3_ = bf16[3072,128]{1,0:T(8,128)(2,1)S(1)} collective-permute-done((bf16[3072,128]{1,0:T(8,128)(2,1)S(1)}, bf16[3072,128]{1,0:T(8,128)(2,1)S(1)}, u32[]{:S(2)}, u32[]{:S(2)}) %collective-permute-start.4) | collective-permute-done | bytes 786464 | tf_op jit(solution)/shard_map/ppermute | solution.py:215
  68.2 4.2 %collective-permute-done.5.refs_4_ = bf16[3072,128]{1,0:T(8,128)(2,1)S(1)} collective-permute-done((bf16[3072,128]{1,0:T(8,128)(2,1)S(1)}, bf16[3072,128]{1,0:T(8,128)(2,1)S(1)}, u32[]{:S(2)}, u32[]{:S(2)}) %collective-permute-start.5) | collective-permute-done | bytes 786464 | tf_op jit(solution)/shard_map/ppermute | solution.py:215
  72.4 5.7 %collective-permute-start.7 = (bf16[3072,128]{1,0:T(8,128)(2,1)S(1)}, bf16[3072,128]{1,0:T(8,128)(2,1)S(1)}, u32[]{:S(2)}, u32[]{:S(2)}) collective-permute-start(bf16[3072,128]{1,0:T(8,128)(2,1)S(1)} %collective-permute-done.4.refs_3_), channel_id=1, source_target_pairs={{4,8},{8,4},{12,16},{16,12},{20,24},{24,20},{28,32},{32,28},{36,40... | collective-permute-start | bytes 2359304 | tf_op jit(solution)/shard_map/ppermute | solution.py:215
  78.1 1.3 collective-permute-done.8.refs_9_
  79.7 6.0 %forward_group.2.refs_2_ = f32[24,128,128]{2,1,0:T(8,128)S(1)} custom-call(s32[398]{0:T(512)S(1)} %broadcast_add_fusion.plan, s32[14]{0:T(128)S(1)} %pad_add_fusion.spans, bf16[384,128,128]{2,1,0:T(8,128)(2,1)} %tiles.9, bf16[3072,128]{1,0:T(8,128)(2,1)S(1)} %gather_rows.1.refs_0_, bf16[3072,128]{1,0:T(8,128)(2,1)S(1)} %collective-permute-done.2.refs_1_, ...), custom_call_target="tpu_custom_call" | custom-call | flops 629145600 | bytes 4915200 | tf_op jit(solution)/shard_map/forward_group/pallas_call | solution.py:143
  85.7 0.9 copy-done.1
  86.6 2.4 %collective-permute-done.6.refs_0_ = bf16[3072,128]{1,0:T(8,128)(2,1)S(1)} collective-permute-done((bf16[3072,128]{1,0:T(8,128)(2,1)S(1)}, bf16[3072,128]{1,0:T(8,128)(2,1)S(1)}, u32[]{:S(2)}, u32[]{:S(2)}) %collective-permute-start.6) | collective-permute-done | bytes 786464 | tf_op jit(solution)/shard_map/ppermute | solution.py:215
  89.0 4.3 %collective-permute-done.7.refs_1_ = bf16[3072,128]{1,0:T(8,128)(2,1)S(1)} collective-permute-done((bf16[3072,128]{1,0:T(8,128)(2,1)S(1)}, bf16[3072,128]{1,0:T(8,128)(2,1)S(1)}, u32[]{:S(2)}, u32[]{:S(2)}) %collective-permute-start.7) | collective-permute-done | bytes 786464 | tf_op jit(solution)/shard_map/ppermute | solution.py:215
  93.3 4.1 %forward_group.3 = (bf16[12,128,128]{2,1,0:T(8,128)(2,1)}, bf16[12,128,128]{2,1,0:T(8,128)(2,1)S(1)}) custom-call(s32[398]{0:T(512)S(1)} %broadcast_add_fusion.plan, s32[14]{0:T(128)S(1)} %pad_add_fusion.spans, bf16[384,128,128]{2,1,0:T(8,128)(2,1)} %tiles.9, bf16[3072,128]{1,0:T(8,128)(2,1)S(1)} %collective-permute-done.6.refs_0_, ...), custom_call_target="tpu_custom_call" | custom-call | flops 251658240 | bytes 1966080 | tf_op jit(solution)/shard_map/forward_group/pallas_call | solution.py:143
  98.1 2.9 %collective-permute-start.13 = (bf16[1536,128]{1,0:T(8,128)(2,1)}, bf16[1536,128]{1,0:T(8,128)(2,1)}, u32[]{:S(2)}, u32[]{:S(2)}) collective-permute-start(bf16[1536,128]{1,0:T(8,128)(2,1)} %bitcast.1.refs_0_), channel_id=1, source_target_pairs={{0,2},{1,3},{2,0},{3,1},{4,6},{5,7},{6,4},{7,5},{8,10},{9,11},{10,... | collective-permute-start | bytes 1179656 | tf_op jit(solution)/shard_map/ppermute | solution.py:220
  101.0 0.8 copy-done.11
  101.8 8.6 %collective-permute-done.16.refs_2_ = bf16[1536,128]{1,0:T(8,128)(2,1)} collective-permute-done((bf16[1536,128]{1,0:T(8,128)(2,1)S(1)}, bf16[1536,128]{1,0:T(8,128)(2,1)}, u32[]{:S(2)}, u32[]{:S(2)}) %collective-permute-start.16) | collective-permute-done | bytes 393248 | tf_op jit(solution)/shard_map/ppermute | solution.py:220
  110.9 3.7 %collective-permute-done.13.refs_2_ = bf16[1536,128]{1,0:T(8,128)(2,1)} collective-permute-done((bf16[1536,128]{1,0:T(8,128)(2,1)}, bf16[1536,128]{1,0:T(8,128)(2,1)}, u32[]{:S(2)}, u32[]{:S(2)}) %collective-permute-start.13) | collective-permute-done | bytes 393248 | tf_op jit(solution)/shard_map/ppermute | solution.py:220
  114.7 1.1 copy-done.2
  115.8 1.0 copy-done.12
  116.8 3.9 %mix.3 = (bf16[1536,128]{1,0:T(8,128)(2,1)S(1)}, bf16[12,128,128]{2,1,0:T(8,128)(2,1)S(1)}, f32[4,128,128]{2,1,0:T(8,128)S(1)}) custom-call(s32[1]{0:T(128)} %bitcast.shard, bf16[1536,128]{1,0:T(8,128)(2,1)S(1)} %bitcast.14, bf16[1536,128]{1,0:T(8,128)(2,1)} %collective-permute-done.15.refs_1_, bf16[1536,128]{1,0:T(8,128)(2,1)} %collective-permute-done.16.refs_2_, ...), custom_call_target="tpu_custom_call" | custom-call | flops 1207959552 | bytes 6291456 | tf_op jit(solution)/shard_map/mix/pallas_call | solution.py:290
  121.4 1.0 copy-done.6
  122.5 4.1 %mix.2 = (bf16[1536,128]{1,0:T(8,128)(2,1)S(1)}, bf16[12,128,128]{2,1,0:T(8,128)(2,1)S(1)}, f32[4,128,128]{2,1,0:T(8,128)S(1)}) custom-call(s32[1]{0:T(128)} %bitcast.shard, bf16[1536,128]{1,0:T(8,128)(2,1)} %bitcast.1.refs_0_, bf16[1536,128]{1,0:T(8,128)(2,1)} %collective-permute-done.12.refs_1_, bf16[1536,128]{1,0:T(8,128)(2,1)} %collective-permute-done.13.refs_2_, ...), custom_call_target="tpu_custom_call" | custom-call | flops 1207959552 | bytes 6291456 | tf_op jit(solution)/shard_map/mix/pallas_call | solution.py:290
  126.6 4.4 %backward_group.3 = (bf16[24,128,128]{2,1,0:T(8,128)(2,1)}, bf16[24,128,128]{2,1,0:T(8,128)(2,1)S(1)}) custom-call(s32[398]{0:T(512)S(1)} %broadcast_add_fusion.plan, s32[14]{0:T(128)S(1)} %copy-done.14, bf16[384,128,128]{2,1,0:T(8,128)(2,1)} %tiles.9, bf16[12,128,128]{2,1,0:T(8,128)(2,1)S(1)} %get-tuple-element.61.refs_0_, ...), custom_call_target="tpu_custom_call" | custom-call | flops 251658240 | bytes 1966080 | tf_op jit(solution)/shard_map/backward_group/pallas_call | solution.py:191
  131.1 5.8 %collective-permute-start.19 = (bf16[24,128,128]{2,1,0:T(8,128)(2,1)S(1)}, bf16[24,128,128]{2,1,0:T(8,128)(2,1)S(1)}, u32[]{:S(2)}, u32[]{:S(2)}) collective-permute-start(bf16[24,128,128]{2,1,0:T(8,128)(2,1)S(1)} %get-tuple-element.65), channel_id=1, source_target_pairs={{4,8},{8,4},{12,16},{16,12},{20,24},{24,20},{28,32},{32,28},{36,40... | collective-permute-start | bytes 2359304 | tf_op jit(solution)/shard_map/ppermute | solution.py:215
  136.9 0.7 add.70
  137.6 5.1 %all-to-all-start = ((f32[64,8,128]{2,1,0:T(8,128)}), f32[64,8,128]{2,1,0:T(8,128)S(1)}, u32[]{:S(2)}, u32[]{:S(2)}) async-start(f32[64,8,128]{2,1,0:T(8,128)} %bitcast.3), calls=%async_computation | async-start | bytes 524288 | tf_op jit(solution)/shard_map/all_to_all | solution.py:357
  142.7 3.3 %backward_group.4 = (bf16[24,128,128]{2,1,0:T(8,128)(2,1)S(1)}, bf16[24,128,128]{2,1,0:T(8,128)(2,1)S(1)}) custom-call(s32[398]{0:T(512)S(1)} %broadcast_add_fusion.plan, s32[14]{0:T(128)S(1)} %copy-done.15, bf16[384,128,128]{2,1,0:T(8,128)(2,1)} %tiles.9, bf16[12,128,128]{2,1,0:T(8,128)(2,1)S(1)} %get-tuple-element.61.refs_0_, ...), custom_call_target="tpu_custom_call" | custom-call | flops 251658240 | bytes 1966080 | tf_op jit(solution)/shard_map/backward_group/pallas_call | solution.py:191
  146.1 6.9 %collective-permute-done.18.carried = bf16[24,128,128]{2,1,0:T(8,128)(2,1)S(1)} collective-permute-done((bf16[24,128,128]{2,1,0:T(8,128)(2,1)}, bf16[24,128,128]{2,1,0:T(8,128)(2,1)S(1)}, u32[]{:S(2)}, u32[]{:S(2)}) %collective-permute-start.18) | collective-permute-done | bytes 786464 | tf_op jit(solution)/shard_map/ppermute | solution.py:215
  153.0 5.6 %collective-permute-done.19.carried = bf16[24,128,128]{2,1,0:T(8,128)(2,1)S(1)} collective-permute-done((bf16[24,128,128]{2,1,0:T(8,128)(2,1)S(1)}, bf16[24,128,128]{2,1,0:T(8,128)(2,1)S(1)}, u32[]{:S(2)}, u32[]{:S(2)}) %collective-permute-start.19) | collective-permute-done | bytes 786464 | tf_op jit(solution)/shard_map/ppermute | solution.py:215
  158.7 1.1 add_part.6
  159.9 6.8 %collective-permute-start.20 = (bf16[24,128,128]{2,1,0:T(8,128)(2,1)S(1)}, bf16[24,128,128]{2,1,0:T(8,128)(2,1)}, u32[]{:S(2)}, u32[]{:S(2)}) collective-permute-start(bf16[24,128,128]{2,1,0:T(8,128)(2,1)S(1)} %add_part.4), channel_id=1, source_target_pairs={{4,8},{8,4},{12,16},{16,12},{20,24},{24,20},{28,32},{32,28},{36,40... | collective-permute-start | bytes 2359304 | tf_op jit(solution)/shard_map/ppermute | solution.py:215
  166.8 0.7 broadcast_in_dim.69
  167.5 5.2 %all-to-all-start.1 = ((f32[64,8,128]{2,1,0:T(8,128)}), f32[64,8,128]{2,1,0:T(8,128)S(1)}, u32[]{:S(2)}, u32[]{:S(2)}) async-start(f32[64,8,128]{2,1,0:T(8,128)} %broadcast_in_dim.69), calls=%async_computation.1 | async-start | bytes 524288 | tf_op jit(solution)/shard_map/all_to_all | solution.py:362
  172.7 5.1 %backward_group.5 = (f32[24,128,128]{2,1,0:T(8,128)S(1)}, bf16[24,128,128]{2,1,0:T(8,128)(2,1)S(1)}, bf16[24,128,128]{2,1,0:T(8,128)(2,1)S(1)}) custom-call(s32[398]{0:T(512)S(1)} %broadcast_add_fusion.plan, s32[14]{0:T(128)S(1)} %copy-done.15, bf16[384,128,128]{2,1,0:T(8,128)(2,1)} %tiles.9, bf16[12,128,128]{2,1,0:T(8,128)(2,1)S(1)} %get-tuple-element.61.refs_0_, ...), custom_call_target="tpu_custom_call" | custom-call | flops 377487360 | bytes 2949120 | tf_op jit(solution)/shard_map/backward_group/pallas_call | solution.py:191
  177.9 4.1 %collective-permute-done.22.carried = bf16[24,128,128]{2,1,0:T(8,128)(2,1)} collective-permute-done((bf16[24,128,128]{2,1,0:T(8,128)(2,1)}, bf16[24,128,128]{2,1,0:T(8,128)(2,1)}, u32[]{:S(2)}, u32[]{:S(2)}) %collective-permute-start.22) | collective-permute-done | bytes 786464 | tf_op jit(solution)/shard_map/ppermute | solution.py:215
  182.0 2.2 %add_part.7 = bf16[24,128,128]{2,1,0:T(8,128)(2,1)} custom-call(bf16[24,128,128]{2,1,0:T(8,128)(2,1)} %collective-permute-done.22.carried, bf16[24,128,128]{2,1,0:T(8,128)(2,1)S(1)} %get-tuple-element.72.own), custom_call_target="tpu_custom_call" | custom-call | bytes 2359296 | tf_op jit(solution)/shard_map/add_part/pallas_call | solution.py:313
  184.2 6.4 %collective-permute-start.23 = (bf16[24,128,128]{2,1,0:T(8,128)(2,1)}, bf16[24,128,128]{2,1,0:T(8,128)(2,1)S(1)}, u32[]{:S(2)}, u32[]{:S(2)}) collective-permute-start(bf16[24,128,128]{2,1,0:T(8,128)(2,1)} %add_part.7), channel_id=1, source_target_pairs={{4,8},{8,4},{12,16},{16,12},{20,24},{24,20},{28,32},{32,28},{36,40... | collective-permute-start | bytes 2359304 | tf_op jit(solution)/shard_map/ppermute | solution.py:215
  190.6 2.2 %add_part.5 = bf16[24,128,128]{2,1,0:T(8,128)(2,1)} custom-call(bf16[24,128,128]{2,1,0:T(8,128)(2,1)} %collective-permute-done.20.carried, bf16[24,128,128]{2,1,0:T(8,128)(2,1)S(1)} %get-tuple-element.69.own), custom_call_target="tpu_custom_call" | custom-call | bytes 2359296 | tf_op jit(solution)/shard_map/add_part/pallas_call | solution.py:313
  192.8 0.9 pad_maximum_fusion
  194.5 12.8 %collective-permute-done.23.right = bf16[24,128,128]{2,1,0:T(8,128)(2,1)S(1)} collective-permute-done((bf16[24,128,128]{2,1,0:T(8,128)(2,1)}, bf16[24,128,128]{2,1,0:T(8,128)(2,1)S(1)}, u32[]{:S(2)}, u32[]{:S(2)}) %collective-permute-start.23) | collective-permute-done | bytes 786464 | tf_op jit(solution)/shard_map/ppermute | solution.py:215
  207.3 1.8 collective-permute-done.21.left
  209.0 5.1 %scatter_rows.1 = bf16[3072,128]{1,0:T(8,128)(2,1)} custom-call(s32[3072]{0:T(1024)S(1)} %broadcast_subtract_fusion.perm, f32[24,128,128]{2,1,0:T(8,128)S(1)} %get-tuple-element.76.own, bf16[24,128,128]{2,1,0:T(8,128)(2,1)S(1)} %collective-permute-done.21.left, bf16[24,128,128]{2,1,0:T(8,128)(2,1)S(1)} %collective-permute-done.23.right), custom_call_target="tpu_custom_call" | custom-call | bytes 12582912 | tf_op jit(solution)/shard_map/scatter_rows/pallas_call | solution.py:343
  (72 shorter events, 5.3 us)
Async XLA Ops:
  0.6 56.0 %copy-start = (bf16[3072,128]{1,0:T(8,128)(2,1)S(1)}, bf16[3072,128]{1,0:T(8,128)(2,1)}, u32[]{:S(2)}) copy-start(bf16[3072,128]{1,0:T(8,128)(2,1)} %refs_4_.1) | copy-start | bytes 2359300
  0.6 23.9 %collective-permute-start = (bf16[3072,128]{1,0:T(8,128)(2,1)}, bf16[3072,128]{1,0:T(8,128)(2,1)S(1)}, u32[]{:S(2)}, u32[]{:S(2)}) collective-permute-start(bf16[3072,128]{1,0:T(8,128)(2,1)} %refs_4_.1), channel_id=1, source_target_pairs={{0,2},{1,3},{2,0},{3,1},{4,6},{5,7},{6,4},{7,5},{8,10},{9,11},{10,... | collective-permute-start | bytes 2359304 | tf_op jit(solution)/shard_map/ppermute | solution.py:220
  2.8 21.7 %collective-permute-start.1 = (bf16[128,512]{1,0:T(8,128)(2,1)}, bf16[128,512]{1,0:T(8,128)(2,1)S(1)}, u32[]{:S(2)}, u32[]{:S(2)}) collective-permute-start(bf16[128,512]{1,0:T(8,128)(2,1)} %refs_8_.1), channel_id=1, source_target_pairs={{0,2},{1,3},{2,0},{3,1},{4,6},{5,7},{6,4},{7,5},{8,10},{9,11},{10,... | collective-permute-start | bytes 393224 | tf_op jit(solution)/shard_map/ppermute | solution.py:220
  5.0 1.1 copy-start.3
  6.1 4.2 %copy-start.16 = (s32[384]{0:T(512)S(1)}, s32[384]{0:T(512)}, u32[]{:S(2)}) copy-start(s32[384]{0:T(512)} %param.9) | copy-start | bytes 4612
  6.1 4.2 %copy-start.17 = (s32[384]{0:T(512)S(1)}, s32[384]{0:T(512)}, u32[]{:S(2)}) copy-start(s32[384]{0:T(512)} %param.10) | copy-start | bytes 4612
  6.1 72.0 %copy-start.4 = (bf16[128,512]{1,0:T(8,128)(2,1)S(1)}, bf16[128,512]{1,0:T(8,128)(2,1)}, u32[]{:S(2)}) copy-start(bf16[128,512]{1,0:T(8,128)(2,1)} %refs_8_.1) | copy-start | bytes 393220
  24.5 18.6 %collective-permute-start.2 = (bf16[3072,128]{1,0:T(8,128)(2,1)S(1)}, bf16[3072,128]{1,0:T(8,128)(2,1)S(1)}, u32[]{:S(2)}, u32[]{:S(2)}) collective-permute-start(bf16[3072,128]{1,0:T(8,128)(2,1)S(1)} %gather_rows.1.refs_0_), channel_id=1, source_target_pairs={{0,4},{4,0},{8,12},{12,8},{16,20},{20,16},{24,28},{28,24},{32,36},... | collective-permute-start | bytes 2359304 | tf_op jit(solution)/shard_map/ppermute | solution.py:215
  26.5 24.2 %collective-permute-start.3 = (bf16[3072,128]{1,0:T(8,128)(2,1)S(1)}, bf16[3072,128]{1,0:T(8,128)(2,1)S(1)}, u32[]{:S(2)}, u32[]{:S(2)}) collective-permute-start(bf16[3072,128]{1,0:T(8,128)(2,1)S(1)} %gather_rows.1.refs_0_), channel_id=1, source_target_pairs={{4,8},{8,4},{12,16},{16,12},{20,24},{24,20},{28,32},{32,28},{36,40... | collective-permute-start | bytes 2359304 | tf_op jit(solution)/shard_map/ppermute | solution.py:215
  50.7 17.5 %collective-permute-start.4 = (bf16[3072,128]{1,0:T(8,128)(2,1)S(1)}, bf16[3072,128]{1,0:T(8,128)(2,1)S(1)}, u32[]{:S(2)}, u32[]{:S(2)}) collective-permute-start(bf16[3072,128]{1,0:T(8,128)(2,1)S(1)} %collective-permute-done.3.refs_2_), channel_id=1, source_target_pairs={{0,4},{4,0},{8,12},{12,8},{16,20},{20,16},{24,28},{28,24},{32,36},... | collective-permute-start | bytes 2359304 | tf_op jit(solution)/shard_map/ppermute | solution.py:215
  50.7 21.7 %collective-permute-start.5 = (bf16[3072,128]{1,0:T(8,128)(2,1)S(1)}, bf16[3072,128]{1,0:T(8,128)(2,1)S(1)}, u32[]{:S(2)}, u32[]{:S(2)}) collective-permute-start(bf16[3072,128]{1,0:T(8,128)(2,1)S(1)} %collective-permute-done.2.refs_1_), channel_id=1, source_target_pairs={{4,8},{8,4},{12,16},{16,12},{20,24},{24,20},{28,32},{32,28},{36,40... | collective-permute-start | bytes 2359304 | tf_op jit(solution)/shard_map/ppermute | solution.py:215
  56.7 29.0 %collective-permute-start.10 = (bf16[3072,128]{1,0:T(8,128)(2,1)S(1)}, bf16[3072,128]{1,0:T(8,128)(2,1)S(1)}, u32[]{:S(2)}, u32[]{:S(2)}) collective-permute-start(bf16[3072,128]{1,0:T(8,128)(2,1)S(1)} %copy-done), channel_id=1, source_target_pairs={{0,1},{1,0},{2,3},{3,2},{4,5},{5,4},{6,7},{7,6},{8,9},{9,8},{10,11... | collective-permute-start | bytes 2359304 | tf_op jit(solution)/shard_map/ppermute | solution.py:220
  56.7 29.0 %collective-permute-start.11 = (bf16[3072,128]{1,0:T(8,128)(2,1)S(1)}, bf16[3072,128]{1,0:T(8,128)(2,1)S(1)}, u32[]{:S(2)}, u32[]{:S(2)}) collective-permute-start(bf16[3072,128]{1,0:T(8,128)(2,1)S(1)} %collective-permute-done.refs_6_), channel_id=1, source_target_pairs={{0,1},{1,0},{2,3},{3,2},{4,5},{5,4},{6,7},{7,6},{8,9},{9,8},{10,11... | collective-permute-start | bytes 2359304 | tf_op jit(solution)/shard_map/ppermute | solution.py:220
  72.4 16.6 %collective-permute-start.6 = (bf16[3072,128]{1,0:T(8,128)(2,1)S(1)}, bf16[3072,128]{1,0:T(8,128)(2,1)S(1)}, u32[]{:S(2)}, u32[]{:S(2)}) collective-permute-start(bf16[3072,128]{1,0:T(8,128)(2,1)S(1)} %collective-permute-done.5.refs_4_), channel_id=1, source_target_pairs={{0,4},{4,0},{8,12},{12,8},{16,20},{20,16},{24,28},{28,24},{32,36},... | collective-permute-start | bytes 2359304 | tf_op jit(solution)/shard_map/ppermute | solution.py:215
  72.4 20.9 %collective-permute-start.7 = (bf16[3072,128]{1,0:T(8,128)(2,1)S(1)}, bf16[3072,128]{1,0:T(8,128)(2,1)S(1)}, u32[]{:S(2)}, u32[]{:S(2)}) collective-permute-start(bf16[3072,128]{1,0:T(8,128)(2,1)S(1)} %collective-permute-done.4.refs_3_), channel_id=1, source_target_pairs={{4,8},{8,4},{12,16},{16,12},{20,24},{24,20},{28,32},{32,28},{36,40... | collective-permute-start | bytes 2359304 | tf_op jit(solution)/shard_map/ppermute | solution.py:215
  78.1 1.3 collective-permute-start.8
  79.5 6.2 %collective-permute-start.9 = (bf16[128,512]{1,0:T(8,128)(2,1)S(1)}, bf16[128,512]{1,0:T(8,128)(2,1)S(1)}, u32[]{:S(2)}, u32[]{:S(2)}) collective-permute-start(bf16[128,512]{1,0:T(8,128)(2,1)S(1)} %collective-permute-done.1.refs_10_), channel_id=1, source_target_pairs={{0,1},{1,0},{2,3},{3,2},{4,5},{5,4},{6,7},{7,6},{8,9},{9,8},{10,11... | collective-permute-start | bytes 393224 | tf_op jit(solution)/shard_map/ppermute | solution.py:220
  79.7 13.6 %copy-start.13 = (s32[14]{0:T(128)}, s32[14]{0:T(128)S(1)}, u32[]{:S(2)}) copy-start(s32[14]{0:T(128)S(1)} %pad_add_fusion.spans) | copy-start | bytes 172
  85.7 0.9 copy-start.1
  97.4 13.0 %collective-permute-start.16 = (bf16[1536,128]{1,0:T(8,128)(2,1)S(1)}, bf16[1536,128]{1,0:T(8,128)(2,1)}, u32[]{:S(2)}, u32[]{:S(2)}) collective-permute-start(bf16[1536,128]{1,0:T(8,128)(2,1)S(1)} %bitcast.12), channel_id=1, source_target_pairs={{0,2},{1,3},{2,0},{3,1},{4,6},{5,7},{6,4},{7,5},{8,10},{9,11},{10,... | collective-permute-start | bytes 1179656 | tf_op jit(solution)/shard_map/ppermute | solution.py:220
  98.1 16.5 %collective-permute-start.13 = (bf16[1536,128]{1,0:T(8,128)(2,1)}, bf16[1536,128]{1,0:T(8,128)(2,1)}, u32[]{:S(2)}, u32[]{:S(2)}) collective-permute-start(bf16[1536,128]{1,0:T(8,128)(2,1)} %bitcast.1.refs_0_), channel_id=1, source_target_pairs={{0,2},{1,3},{2,0},{3,1},{4,6},{5,7},{6,4},{7,5},{8,10},{9,11},{10,... | collective-permute-start | bytes 1179656 | tf_op jit(solution)/shard_map/ppermute | solution.py:220
  101.0 13.6 %collective-permute-start.15 = (bf16[1536,128]{1,0:T(8,128)(2,1)S(1)}, bf16[1536,128]{1,0:T(8,128)(2,1)}, u32[]{:S(2)}, u32[]{:S(2)}) collective-permute-start(bf16[1536,128]{1,0:T(8,128)(2,1)S(1)} %bitcast.13), channel_id=1, source_target_pairs={{0,1},{1,0},{2,3},{3,2},{4,5},{5,4},{6,7},{7,6},{8,9},{9,8},{10,11... | collective-permute-start | bytes 1179656 | tf_op jit(solution)/shard_map/ppermute | solution.py:220
  101.0 0.8 copy-start.11
  110.4 4.2 %collective-permute-start.17 = (bf16[1536,128]{1,0:T(8,128)(2,1)}, bf16[1536,128]{1,0:T(8,128)(2,1)}, u32[]{:S(2)}, u32[]{:S(2)}) collective-permute-start(bf16[1536,128]{1,0:T(8,128)(2,1)} %collective-permute-done.16.refs_2_), channel_id=1, source_target_pairs={{0,1},{1,0},{2,3},{3,2},{4,5},{5,4},{6,7},{7,6},{8,9},{9,8},{10,11... | collective-permute-start | bytes 1179656 | tf_op jit(solution)/shard_map/ppermute | solution.py:220
  110.4 11.0 %collective-permute-start.12 = (bf16[1536,128]{1,0:T(8,128)(2,1)}, bf16[1536,128]{1,0:T(8,128)(2,1)}, u32[]{:S(2)}, u32[]{:S(2)}) collective-permute-start(bf16[1536,128]{1,0:T(8,128)(2,1)} %bitcast.1.refs_0_), channel_id=1, source_target_pairs={{0,1},{1,0},{2,3},{3,2},{4,5},{5,4},{6,7},{7,6},{8,9},{9,8},{10,11... | collective-permute-start | bytes 1179656 | tf_op jit(solution)/shard_map/ppermute | solution.py:220
  114.6 6.8 %collective-permute-start.14 = (bf16[1536,128]{1,0:T(8,128)(2,1)}, bf16[1536,128]{1,0:T(8,128)(2,1)}, u32[]{:S(2)}, u32[]{:S(2)}) collective-permute-start(bf16[1536,128]{1,0:T(8,128)(2,1)} %collective-permute-done.13.refs_2_), channel_id=1, source_target_pairs={{0,1},{1,0},{2,3},{3,2},{4,5},{5,4},{6,7},{7,6},{8,9},{9,8},{10,11... | collective-permute-start | bytes 1179656 | tf_op jit(solution)/shard_map/ppermute | solution.py:220
  114.7 1.1 copy-start.2
  115.8 1.0 copy-start.12
  116.8 9.8 %copy-start.14 = (s32[14]{0:T(128)S(1)}, s32[14]{0:T(128)}, u32[]{:S(2)}) copy-start(s32[14]{0:T(128)} %copy-done.13) | copy-start | bytes 172
  120.7 0.7 copy-start.5
  121.4 5.1 %copy-start.7 = (bf16[1536,128]{1,0:T(8,128)(2,1)}, bf16[1536,128]{1,0:T(8,128)(2,1)S(1)}, u32[]{:S(2)}) copy-start(bf16[1536,128]{1,0:T(8,128)(2,1)S(1)} %get-tuple-element.74) | copy-start | bytes 1179652
  121.4 1.0 copy-start.6
  126.5 4.4 %copy-start.9 = (bf16[1536,128]{1,0:T(8,128)(2,1)}, bf16[1536,128]{1,0:T(8,128)(2,1)S(1)}, u32[]{:S(2)}) copy-start(bf16[1536,128]{1,0:T(8,128)(2,1)S(1)} %get-tuple-element.73) | copy-start | bytes 1179652
  126.6 16.2 %copy-start.15 = (s32[14]{0:T(128)S(1)}, s32[14]{0:T(128)}, u32[]{:S(2)}) copy-start(s32[14]{0:T(128)} %copy-done.13) | copy-start | bytes 172
  131.0 22.0 %collective-permute-start.18 = (bf16[24,128,128]{2,1,0:T(8,128)(2,1)}, bf16[24,128,128]{2,1,0:T(8,128)(2,1)S(1)}, u32[]{:S(2)}, u32[]{:S(2)}) collective-permute-start(bf16[24,128,128]{2,1,0:T(8,128)(2,1)} %get-tuple-element.64), channel_id=1, source_target_pairs={{0,4},{4,0},{8,12},{12,8},{16,20},{20,16},{24,28},{28,24},{32,36},... | collective-permute-start | bytes 2359304 | tf_op jit(solution)/shard_map/ppermute | solution.py:215
  131.1 27.6 %collective-permute-start.19 = (bf16[24,128,128]{2,1,0:T(8,128)(2,1)S(1)}, bf16[24,128,128]{2,1,0:T(8,128)(2,1)S(1)}, u32[]{:S(2)}, u32[]{:S(2)}) collective-permute-start(bf16[24,128,128]{2,1,0:T(8,128)(2,1)S(1)} %get-tuple-element.65), channel_id=1, source_target_pairs={{4,8},{8,4},{12,16},{16,12},{20,24},{24,20},{28,32},{32,28},{36,40... | collective-permute-start | bytes 2359304 | tf_op jit(solution)/shard_map/ppermute | solution.py:215
  137.6 29.1 %all-to-all-start = ((f32[64,8,128]{2,1,0:T(8,128)}), f32[64,8,128]{2,1,0:T(8,128)S(1)}, u32[]{:S(2)}, u32[]{:S(2)}) async-start(f32[64,8,128]{2,1,0:T(8,128)} %bitcast.3), calls=%async_computation | async-start | bytes 524288 | tf_op jit(solution)/shard_map/all_to_all | solution.py:357
  159.7 22.2 %collective-permute-start.22 = (bf16[24,128,128]{2,1,0:T(8,128)(2,1)}, bf16[24,128,128]{2,1,0:T(8,128)(2,1)}, u32[]{:S(2)}, u32[]{:S(2)}) collective-permute-start(bf16[24,128,128]{2,1,0:T(8,128)(2,1)} %add_part.6), channel_id=1, source_target_pairs={{0,4},{4,0},{8,12},{12,8},{16,20},{20,16},{24,28},{28,24},{32,36},... | collective-permute-start | bytes 2359304 | tf_op jit(solution)/shard_map/ppermute | solution.py:215
  159.9 30.7 %collective-permute-start.20 = (bf16[24,128,128]{2,1,0:T(8,128)(2,1)S(1)}, bf16[24,128,128]{2,1,0:T(8,128)(2,1)}, u32[]{:S(2)}, u32[]{:S(2)}) collective-permute-start(bf16[24,128,128]{2,1,0:T(8,128)(2,1)S(1)} %add_part.4), channel_id=1, source_target_pairs={{4,8},{8,4},{12,16},{16,12},{20,24},{24,20},{28,32},{32,28},{36,40... | collective-permute-start | bytes 2359304 | tf_op jit(solution)/shard_map/ppermute | solution.py:215
  167.5 26.3 %all-to-all-start.1 = ((f32[64,8,128]{2,1,0:T(8,128)}), f32[64,8,128]{2,1,0:T(8,128)S(1)}, u32[]{:S(2)}, u32[]{:S(2)}) async-start(f32[64,8,128]{2,1,0:T(8,128)} %broadcast_in_dim.69), calls=%async_computation.1 | async-start | bytes 524288 | tf_op jit(solution)/shard_map/all_to_all | solution.py:362
  184.2 8.6 %copy-start.8 = (bf16[1536,128]{1,0:T(8,128)(2,1)S(1)}, bf16[1536,128]{1,0:T(8,128)(2,1)}, u32[]{:S(2)}) copy-start(bf16[1536,128]{1,0:T(8,128)(2,1)} %copy-done.7) | copy-start | bytes 1179652
  184.2 8.6 %copy-start.10 = (bf16[1536,128]{1,0:T(8,128)(2,1)S(1)}, bf16[1536,128]{1,0:T(8,128)(2,1)}, u32[]{:S(2)}) copy-start(bf16[1536,128]{1,0:T(8,128)(2,1)} %copy-done.9) | copy-start | bytes 1179652
  184.2 23.1 %collective-permute-start.23 = (bf16[24,128,128]{2,1,0:T(8,128)(2,1)}, bf16[24,128,128]{2,1,0:T(8,128)(2,1)S(1)}, u32[]{:S(2)}, u32[]{:S(2)}) collective-permute-start(bf16[24,128,128]{2,1,0:T(8,128)(2,1)} %add_part.7), channel_id=1, source_target_pairs={{4,8},{8,4},{12,16},{16,12},{20,24},{24,20},{28,32},{32,28},{36,40... | collective-permute-start | bytes 2359304 | tf_op jit(solution)/shard_map/ppermute | solution.py:215
  192.8 16.2 %collective-permute-start.21 = (bf16[24,128,128]{2,1,0:T(8,128)(2,1)}, bf16[24,128,128]{2,1,0:T(8,128)(2,1)S(1)}, u32[]{:S(2)}, u32[]{:S(2)}) collective-permute-start(bf16[24,128,128]{2,1,0:T(8,128)(2,1)} %add_part.5), channel_id=1, source_target_pairs={{0,4},{4,0},{8,12},{12,8},{16,20},{20,16},{24,28},{28,24},{32,36},... | collective-permute-start | bytes 2359304 | tf_op jit(solution)/shard_map/ppermute | solution.py:215
